TPU v7x, 128 devices: a whole 4x4x4 slice. The times are simulated.
128 devices in a mesh: ax: 16 (over x, z_hi, core), xs: 8 (over z_lo, y).
Axes of the slice: x: 4, y: 4, z: 4 (z_hi: 2, z_lo: 2; z = z_hi * 2 + z_lo), core: 2. Of those that a mesh axis runs over, the one named last changes fastest.
Arguments:
- populations: float32 [19, 64, 512, 256], P(None, 'ax', 'xs'), may hold values from 0.001 to 0.75, as said below
- fluid_mask: int32 [64, 512, 256], P('ax', 'xs'), may hold values 0 or 1
- patch_voxel: int32 [1024, 512], P(('ax', 'xs')), may hold values from 0 to 65535
- patch_owner: int32 [1024], P(('ax', 'xs')), may hold values from 0 to 7, as said below
- positions: float32 [1024, 3, 512], P(('ax', 'xs')), may hold values from 0 to 5.5
- velocities: float32 [1024, 3, 512], P(('ax', 'xs')), may hold values from -6 to 6
- pair_tiles: int32 [1024, 8, 2], P(('ax', 'xs')), may hold values from 0 to 3
- pair_noise: bfloat16 [1024, 8, 128, 128], P(('ax', 'xs')), may hold values from -6 to 6
Outputs:
- populations_out: float32 [19, 64, 512, 256], P(None, 'ax', 'xs')
- new_positions: float32 [1024, 3, 512], P(('ax', 'xs'))
- new_velocities: float32 [1024, 3, 512], P(('ax', 'xs'))
- drag_field: float32 [3, 64, 512, 256], P(None, 'ax', 'xs')
Inputs may be any that keep to these rules, and one draw needn't show every extreme that they name: `patch_owner`: among the 8 patches of every device, each index along xs is named exactly 1 times. `populations`: every distribution is positive.
All inputs are finite; a program needn't handle non-finite values. No bound on the sum of `fluid_mask` on one device may be relied on, other than what follows from the above.
Results may differ from a plain program's by a relative error of at most 0.0003.
Values sent between devices are 32-bit elements; how exact they have to be, the bound alone decides.
A program may use at most 128 MiB of HBM per device.

v0:
```python
import jax
import jax.numpy as jnp
from jax import lax
from jax.sharding import PartitionSpec as P

LATTICE_DIRS = [
    (0, 0, 0),
    (1, 0, 0),
    (-1, 0, 0),
    (0, 1, 0),
    (0, -1, 0),
    (0, 0, 1),
    (0, 0, -1),
    (1, 1, 0),
    (-1, -1, 0),
    (1, -1, 0),
    (-1, 1, 0),
    (1, 0, 1),
    (-1, 0, -1),
    (1, 0, -1),
    (-1, 0, 1),
    (0, 1, 1),
    (0, -1, -1),
    (0, 1, -1),
    (0, -1, 1),
]
LATTICE_WEIGHTS = [1.0 / 3.0] + [1.0 / 18.0] * 6 + [1.0 / 36.0] * 12
OPPOSITE_DIR = [0, 2, 1, 4, 3, 6, 5, 8, 7, 10, 9, 12, 11, 14, 13, 16, 15, 18, 17]
RELAX_TIME = 0.8
TIME_STEP = 0.04
REPULSION = 25.0
FRICTION = 4.5
NOISE_AMP = 3.0
DRAG_COEFF = 12.5
VELOCITY_SCALE = 20.0
SOFTENING = 0.01


def padded_2(cells, sides, width, closed):
    for axis, dim in sides:
        count = lax.axis_size(axis)
        ends = count if closed else count - 1
        head = lax.slice_in_dim(cells, 0, width, axis=dim)
        tail = lax.slice_in_dim(cells, cells.shape[dim] - width, cells.shape[dim], axis=dim)
        cells = jnp.concatenate(
            [
                lax.ppermute(tail, axis, [(i, (i + 1) % count) for i in range(ends)]),
                cells,
                lax.ppermute(head, axis, [((i + 1) % count, i) for i in range(ends)]),
            ],
            axis=dim,
        )
    return cells


def moments(dist):
    density = jnp.sum(dist, axis=0)
    comps = []
    for axis in range(3):
        total = jnp.zeros_like(density)
        for index in range(19):
            sign = LATTICE_DIRS[index][axis]
            if sign != 0:
                total = total + sign * dist[index]
        comps.append(total / density)
    return (density, comps)


def collide(dist):
    density, comps = moments(dist)
    speed_sq = comps[0] * comps[0] + comps[1] * comps[1] + comps[2] * comps[2]
    out = []
    for index in range(19):
        dirx, diry, dirz = LATTICE_DIRS[index]
        proj = dirx * comps[0] + diry * comps[1] + dirz * comps[2]
        equil = (
            LATTICE_WEIGHTS[index]
            * density
            * (1.0 + 3.0 * proj + 4.5 * proj * proj - 1.5 * speed_sq)
        )
        out.append(dist[index] - (dist[index] - equil) / RELAX_TIME)
    return jnp.stack(out)


def stream_padded(padded, post):
    size_x, size_y, size_z = (post.shape[1], post.shape[2], post.shape[3])
    out = []
    for index in range(19):
        dirx, diry, dirz = LATTICE_DIRS[index]
        start_x, start_y, start_z = (1 - dirx, 1 - diry, 1 - dirz)
        source = padded[
            index,
            start_x : start_x + size_x,
            start_y : start_y + size_y,
            start_z : start_z + size_z,
        ]
        source_mask = padded[
            19, start_x : start_x + size_x, start_y : start_y + size_y, start_z : start_z + size_z
        ]
        out.append(jnp.where(source_mask > 0.5, source, post[OPPOSITE_DIR[index]]))
    return jnp.stack(out)


def pad_depth(block):
    return jnp.pad(block, ((0, 0), (0, 0), (0, 0), (1, 1)))


def lattice_step(dist, fluid):
    post = collide(dist)
    stacked = jnp.concatenate([post, fluid[None]], axis=0)
    axial = padded_2(stacked, (("ax", 1),), 1, True)
    full = padded_2(axial, (("xs", 2),), 1, False)
    return stream_padded(pad_depth(full), post)


def pair_forces(position, velocity, pair_list, noise):
    tile = noise.shape[-1]
    count = position.shape[1] // tile
    pos_tiles = position.reshape(3, count, tile)
    vel_tiles = velocity.reshape(3, count, tile)

    def one_pair(carry, item):
        pair, noise_tile = item
        pos_a = lax.dynamic_index_in_dim(pos_tiles, pair[0], 1, keepdims=False)
        pos_b = lax.dynamic_index_in_dim(pos_tiles, pair[1], 1, keepdims=False)
        vel_a = lax.dynamic_index_in_dim(vel_tiles, pair[0], 1, keepdims=False)
        vel_b = lax.dynamic_index_in_dim(vel_tiles, pair[1], 1, keepdims=False)
        delta = pos_a[:, :, None] - pos_b[:, None, :]
        distance = jnp.sqrt(jnp.sum(delta * delta, axis=0) + SOFTENING)
        weight = jnp.maximum(0.0, 1.0 - distance)
        unit = delta / distance
        along = jnp.sum(unit * (vel_a[:, :, None] - vel_b[:, None, :]), axis=0)
        scalar = (
            REPULSION * weight
            - FRICTION * weight * weight * along
            + NOISE_AMP * weight * noise_tile.astype(jnp.float32) / jnp.sqrt(TIME_STEP)
        )
        force = jnp.sum(scalar[None] * unit, axis=2)
        current = lax.dynamic_index_in_dim(carry, pair[0], 1, keepdims=False)
        carry = lax.dynamic_update_index_in_dim(carry, current + force, pair[0], 1)
        return (carry, None)

    start = jnp.zeros((3, count, tile), jnp.float32)
    total, unused = lax.scan(one_pair, start, (pair_list, noise))
    return total.reshape(3, count * tile)


def patch_step(item):
    position, velocity, flow, pair_list, noise = item
    drag = DRAG_COEFF * (flow - velocity)
    new_vel = velocity + TIME_STEP * (pair_forces(position, velocity, pair_list, noise) + drag)
    new_pos = position + TIME_STEP * new_vel
    return (new_pos, new_vel, -TIME_STEP * drag)


def per_device(
    populations, fluid_mask, patch_voxel, patch_owner, positions, velocities, pair_tiles, pair_noise
):
    fluid = fluid_mask.astype(jnp.float32)
    dist = populations
    for step in range(2):
        dist = lattice_step(dist, fluid)
    density, comps = moments(dist)
    cells = dist.shape[1] * dist.shape[2] * dist.shape[3]
    velocity_flat = VELOCITY_SCALE * jnp.stack(comps).reshape(3, cells)
    patch_count, bead_count = patch_voxel.shape
    owners = lax.axis_size("xs")
    share = patch_count // owners
    at_beads = jnp.transpose(velocity_flat[:, patch_voxel], (1, 0, 2))
    order = jnp.argsort(patch_owner, stable=True)
    grouped = at_beads[order].reshape(owners, share, 3, bead_count)
    received = lax.all_to_all(grouped, "xs", split_axis=0, concat_axis=0, tiled=True).reshape(
        patch_count, 3, bead_count
    )
    new_pos, new_vel, reaction = lax.map(
        patch_step, (positions, velocities, received, pair_tiles, pair_noise)
    )
    returned = lax.all_to_all(
        reaction.reshape(owners, share, 3, bead_count),
        "xs",
        split_axis=0,
        concat_axis=0,
        tiled=True,
    )
    returned = returned.reshape(patch_count, 3, bead_count)
    back = returned[jnp.argsort(order)]
    flat_ids = patch_voxel.reshape(-1)
    field = jnp.stack(
        [
            jax.ops.segment_sum(back[:, comp, :].reshape(-1), flat_ids, num_segments=cells)
            for comp in range(3)
        ]
    )
    return (dist, new_pos, new_vel, field.reshape(3, dist.shape[1], dist.shape[2], dist.shape[3]))


def solution(mesh):
    return jax.shard_map(
        per_device,
        mesh=mesh,
        in_specs=(
            P(None, "ax", "xs", None),
            P("ax", "xs", None),
            P(("ax", "xs"), None),
            P(("ax", "xs")),
            P(("ax", "xs"), None, None),
            P(("ax", "xs"), None, None),
            P(("ax", "xs"), None, None),
            P(("ax", "xs"), None, None, None),
        ),
        out_specs=(
            P(None, "ax", "xs", None),
            P(("ax", "xs"), None, None),
            P(("ax", "xs"), None, None),
            P(None, "ax", "xs", None),
        ),
        check_vma=False,
    )
```

profile of v0, /device:TPU:1, one launch (start us, length us, event | category | flops | bytes accessed | tf_op | source)
XLA Modules:
  0.0 693.2 jit_solution(12507339520125347113)
XLA Ops:
  0.6 2.8 reduce_sum.2318
  3.4 3.8 constant_dynamic-update-slice_fusion.18
  17.2 5.1 collective-permute-start
  22.2 30.2 %collective-permute-done = f32[20,1,64,256]{3,2,1,0:T(8,128)S(1)} collective-permute-done((f32[20,1,64,256]{3,2,1,0:T(8,128)S(1)}, f32[20,1,64,256]{3,2,1,0:T(8,128)S(1)}, u32[]{:S(2)}, u32[]{:S(2)}) %collective-permute-start) | collective-permute-done | bytes 1310752 | tf_op jit(solution)/shard_map/ppermute | solution.py:47
  52.4 2.1 collective-permute-done.1
  58.5 3.7 collective-permute-done.3
  62.4 8.1 %select_maximum_fusion.4 = f32[20,6,66,258]{3,2,1,0:T(8,128)S(1)} fusion(f32[20,6,1,256]{3,2,1,0:T(1,128)S(1)} %copy.136, f32[20,6,1,256]{3,2,1,0:T(1,128)S(1)} %copy.134, f32[20,1,64,256]{3,2,1,0:T(8,128)S(1)} %collective-permute-done.1, f32[20,4,64,256]{3,2,1,0:T(8,128)S(1)} %bitcast_dynamic-update-slice_fusion.1, ...), kind=kLoop, calls=%fused_computation.48 | loop fusion | flops 24520320 | bytes 16283520 | tf_op jit(solution)/shard_map/concatenate | solution.py:45
  70.5 5.3 constant_dynamic-update-slice_fusion.37
  94.0 2.3 copy-done
  98.0 3.3 collective-permute-start.4
  103.4 29.1 %collective-permute-done.5 = f32[20,1,64,256]{3,2,1,0:T(8,128)S(1)} collective-permute-done((f32[20,1,64,256]{3,2,1,0:T(8,128)}, f32[20,1,64,256]{3,2,1,0:T(8,128)S(1)}, u32[]{:S(2)}, u32[]{:S(2)}) %collective-permute-start.5) | collective-permute-done | bytes 1310752 | tf_op jit(solution)/shard_map/ppermute | solution.py:49
  135.3 4.6 collective-permute-start.6
  142.7 11.6 %select_maximum_fusion = f32[20,6,66,258]{3,2,1,0:T(8,128)} fusion(f32[20,6,1,256]{3,2,1,0:T(1,128)S(1)} %copy.142, f32[20,6,1,256]{3,2,1,0:T(1,128)S(1)} %copy.140, f32[20,1,64,256]{3,2,1,0:T(8,128)S(1)} %collective-permute-done.5, f32[20,4,64,256]{3,2,1,0:T(8,128)} %copy-done, f32[20,1,64,256]{3,2,1,0:T(8,128)S(1)} %collective-permute-done.4), kind=kLoop, calls=%fused_computation.44 | loop fusion | flops 24520320 | bytes 16283520 | tf_op jit(solution)/shard_map/concatenate | solution.py:45
  154.2 8.4 %add_divide_fusion.2 = (f32[1,4,64,256]{3,2,1,0:T(8,128)}, f32[1,4,64,256]{3,2,1,0:T(8,128)}, f32[1,4,64,256]{3,2,1,0:T(8,128)S(1)}, f32[1,4,64,256]{3,2,1,0:T(8...) fusion(f32[1,4,64,256]{3,2,1,0:T(8,128)S(1)} %get-tuple-element, ...), kind=kLoop, calls=%fused_computation.420 | loop fusion | flops 7143424 | bytes 23576576 | tf_op jit(solution)/shard_map/div | solution.py:65
  186.0 15.9 %copy.145 = f32[3,65536]{0,1:T(8,128)} copy(f32[3,65536]{1,0:T(4,128)S(1)} %maximum_multiply_fusion) | data formatting | bytes 1572864 | tf_op jit(solution)/shard_map/mul | solution.py:165
  201.9 21.3 %gather_fusion = f32[4096,3]{1,0:T(8,128)S(1)} fusion(f32[3,65536]{0,1:T(8,128)} %copy.145, s32[4096]{0:T(1024)S(1)} %broadcast_clamp_fusion), kind=kCustom, calls=%fused_computation | custom fusion | bytes 114688 | tf_op jit(solution)/shard_map/gather | solution.py:169
  225.1 7.9 %all-to-all-start = ((f32[8,1,3,512]{3,1,2,0:T(1,128)}), f32[8,1,3,512]{3,1,2,0:T(1,128)S(1)}, u32[]{:S(2)}, u32[]{:S(2)}) async-start(f32[8,1,3,512]{3,1,2,0:T(1,128)} %copy.147), calls=%async_computation | async-start | bytes 98304 | tf_op jit(solution)/shard_map/all_to_all | solution.py:172
  233.8 4.4 all-to-all-done
  238.2 377.4 %while.36 = (s32[]{:T(128)}, f32[8,3,512]{2,0,1:T(8,128)}, f32[8,3,512]{2,0,1:T(8,128)}, f32[8,3,512]{2,1,0:T(4,128)S(1)}, f32[8,3,512]{2,0,1:T(8,128)}, /*index...) while((s32[]{:T(128)}, f32[8,3,512]{2,0,1:T(8,128)}, ...), condition=%wide.region_8.9_spmd, body=%wide.region_2.8_spmd.sunk | while | flops 798730 | bytes 1413218 | solution.py:175
  241.5 40.9 %while.37 = (s32[]{:T(128)}, f32[3,4,128]{2,0,1:T(4,128)S(1)}, s32[8,2]{0,1:T(2,128)S(1)}, f32[3,4,128]{2,0,1:T(4,128)S(1)}, f32[3,4,128]{2,0,1:T(4,128)S(1)}, /...) while((s32[]{:T(128)}, f32[3,4,128]{2,0,1:T(4,128)S(1)}, s32[8,2]{0,1:T(2,128)S(1)}, ...), condition=%wide.region_7.7_spmd, body=%wide.region_3.0_spmd.sunk | while | flops 786440 | bytes 720605 | solution.py:144
  288.7 40.9 %while.37 = (s32[]{:T(128)}, f32[3,4,128]{2,0,1:T(4,128)S(1)}, s32[8,2]{0,1:T(2,128)S(1)}, f32[3,4,128]{2,0,1:T(4,128)S(1)}, f32[3,4,128]{2,0,1:T(4,128)S(1)}, /...) while((s32[]{:T(128)}, f32[3,4,128]{2,0,1:T(4,128)S(1)}, s32[8,2]{0,1:T(2,128)S(1)}, ...), condition=%wide.region_7.7_spmd, body=%wide.region_3.0_spmd.sunk | while | flops 786440 | bytes 720605 | solution.py:144
  335.8 40.9 %while.37 = (s32[]{:T(128)}, f32[3,4,128]{2,0,1:T(4,128)S(1)}, s32[8,2]{0,1:T(2,128)S(1)}, f32[3,4,128]{2,0,1:T(4,128)S(1)}, f32[3,4,128]{2,0,1:T(4,128)S(1)}, /...) while((s32[]{:T(128)}, f32[3,4,128]{2,0,1:T(4,128)S(1)}, s32[8,2]{0,1:T(2,128)S(1)}, ...), condition=%wide.region_7.7_spmd, body=%wide.region_3.0_spmd.sunk | while | flops 786440 | bytes 720605 | solution.py:144
  383.0 40.9 %while.37 = (s32[]{:T(128)}, f32[3,4,128]{2,0,1:T(4,128)S(1)}, s32[8,2]{0,1:T(2,128)S(1)}, f32[3,4,128]{2,0,1:T(4,128)S(1)}, f32[3,4,128]{2,0,1:T(4,128)S(1)}, /...) while((s32[]{:T(128)}, f32[3,4,128]{2,0,1:T(4,128)S(1)}, s32[8,2]{0,1:T(2,128)S(1)}, ...), condition=%wide.region_7.7_spmd, body=%wide.region_3.0_spmd.sunk | while | flops 786440 | bytes 720605 | solution.py:144
  430.2 40.9 %while.37 = (s32[]{:T(128)}, f32[3,4,128]{2,0,1:T(4,128)S(1)}, s32[8,2]{0,1:T(2,128)S(1)}, f32[3,4,128]{2,0,1:T(4,128)S(1)}, f32[3,4,128]{2,0,1:T(4,128)S(1)}, /...) while((s32[]{:T(128)}, f32[3,4,128]{2,0,1:T(4,128)S(1)}, s32[8,2]{0,1:T(2,128)S(1)}, ...), condition=%wide.region_7.7_spmd, body=%wide.region_3.0_spmd.sunk | while | flops 786440 | bytes 720605 | solution.py:144
  477.4 40.9 %while.37 = (s32[]{:T(128)}, f32[3,4,128]{2,0,1:T(4,128)S(1)}, s32[8,2]{0,1:T(2,128)S(1)}, f32[3,4,128]{2,0,1:T(4,128)S(1)}, f32[3,4,128]{2,0,1:T(4,128)S(1)}, /...) while((s32[]{:T(128)}, f32[3,4,128]{2,0,1:T(4,128)S(1)}, s32[8,2]{0,1:T(2,128)S(1)}, ...), condition=%wide.region_7.7_spmd, body=%wide.region_3.0_spmd.sunk | while | flops 786440 | bytes 720605 | solution.py:144
  524.5 40.9 %while.37 = (s32[]{:T(128)}, f32[3,4,128]{2,0,1:T(4,128)S(1)}, s32[8,2]{0,1:T(2,128)S(1)}, f32[3,4,128]{2,0,1:T(4,128)S(1)}, f32[3,4,128]{2,0,1:T(4,128)S(1)}, /...) while((s32[]{:T(128)}, f32[3,4,128]{2,0,1:T(4,128)S(1)}, s32[8,2]{0,1:T(2,128)S(1)}, ...), condition=%wide.region_7.7_spmd, body=%wide.region_3.0_spmd.sunk | while | flops 786440 | bytes 720605 | solution.py:144
  571.7 40.9 %while.37 = (s32[]{:T(128)}, f32[3,4,128]{2,0,1:T(4,128)S(1)}, s32[8,2]{0,1:T(2,128)S(1)}, f32[3,4,128]{2,0,1:T(4,128)S(1)}, f32[3,4,128]{2,0,1:T(4,128)S(1)}, /...) while((s32[]{:T(128)}, f32[3,4,128]{2,0,1:T(4,128)S(1)}, s32[8,2]{0,1:T(2,128)S(1)}, ...), condition=%wide.region_7.7_spmd, body=%wide.region_3.0_spmd.sunk | while | flops 786440 | bytes 720605 | solution.py:144
  616.3 3.3 all-to-all-start.1
  620.3 4.4 all-to-all-done.1
  625.4 22.3 %scatter_custom_fusion.2 = f32[65536]{0:T(1024)S(1)} fusion(s32[4096]{0:T(1024)} %bitcast.184, f32[4096]{0:T(1024)S(1)} %bitcast.189, f32[]{:T(128)} %constant.149.clone.1), kind=kCustom, calls=%fused_computation.437 | custom fusion | flops 4096 | bytes 262656 | tf_op jit(solution)/shard_map/scatter-add | solution.py:190
  647.8 22.1 %scatter_custom_fusion.1 = f32[65536]{0:T(1024)S(1)} fusion(s32[4096]{0:T(1024)} %bitcast.185, f32[4096]{0:T(1024)S(1)} %bitcast.188, f32[]{:T(128)} %constant.149.clone.1), kind=kCustom, calls=%fused_computation.439 | custom fusion | flops 4096 | bytes 262656 | tf_op jit(solution)/shard_map/scatter-add | solution.py:190
  670.0 22.1 %scatter_custom_fusion = f32[65536]{0:T(1024)S(1)} fusion(s32[4096]{0:T(1024)} %bitcast.186, f32[4096]{0:T(1024)S(1)} %bitcast.187, f32[]{:T(128)} %constant.149.clone.1), kind=kCustom, calls=%fused_computation.441 | custom fusion | flops 4096 | bytes 262656 | tf_op jit(solution)/shard_map/scatter-add | solution.py:190
  (856 shorter events, 201.2 us)
Async XLA Ops:
  17.2 35.2 %collective-permute-start = (f32[20,1,64,256]{3,2,1,0:T(8,128)S(1)}, f32[20,1,64,256]{3,2,1,0:T(8,128)S(1)}, u32[]{:S(2)}, u32[]{:S(2)}) collective-permute-start(f32[20,1,64,256]{3,2,1,0:T(8,128)S(1)} %get-tuple-element.434), channel_id=1, source_target_pairs={{0,8},{8,16},{16,24},{24,32},{32,40},{40,48},{48,56},{56,64},{64,7... | collective-permute-start | bytes 3932168 | tf_op jit(solution)/shard_map/ppermute | solution.py:47
  22.2 32.3 %collective-permute-start.1 = (f32[20,1,64,256]{3,2,1,0:T(8,128)S(1)}, f32[20,1,64,256]{3,2,1,0:T(8,128)S(1)}, u32[]{:S(2)}, u32[]{:S(2)}) collective-permute-start(f32[20,1,64,256]{3,2,1,0:T(8,128)S(1)} %get-tuple-element.433), channel_id=1, source_target_pairs={{8,0},{16,8},{24,16},{32,24},{40,32},{48,40},{56,48},{64,56},{72,6... | collective-permute-start | bytes 3932168 | tf_op jit(solution)/shard_map/ppermute | solution.py:49
  54.7 3.7 collective-permute-start.2
  56.4 5.9 collective-permute-start.3
  75.7 5.6 copy-start.29
  75.7 6.4 copy-start.28
  75.8 7.3 %copy-start.27 = (f32[1,4,64,256]{3,2,1,0:T(8,128)S(1)}, f32[1,4,64,256]{3,2,1,0:T(8,128)}, u32[]{:S(2)}) copy-start(f32[1,4,64,256]{3,2,1,0:T(8,128)} %get-tuple-element.361) | copy-start | bytes 786436
  77.6 6.3 copy-start.26
  92.3 9.1 %copy-start.33 = (s32[8,512]{1,0:T(8,128)S(1)}, s32[8,512]{1,0:T(8,128)}, u32[]{:S(2)}) copy-start(s32[8,512]{1,0:T(8,128)} %param.14) | copy-start | bytes 49156
  92.3 9.1 %copy-start.34 = (s32[8]{0:T(128)S(1)}, s32[8]{0:T(128)}, u32[]{:S(2)}) copy-start(s32[8]{0:T(128)} %param.15) | copy-start | bytes 100
  98.0 34.5 %collective-permute-start.5 = (f32[20,1,64,256]{3,2,1,0:T(8,128)}, f32[20,1,64,256]{3,2,1,0:T(8,128)S(1)}, u32[]{:S(2)}, u32[]{:S(2)}) collective-permute-start(f32[20,1,64,256]{3,2,1,0:T(8,128)} %get-tuple-element.432), channel_id=1, source_target_pairs={{8,0},{16,8},{24,16},{32,24},{40,32},{48,40},{56,48},{64,56},{72,6... | collective-permute-start | bytes 3932168 | tf_op jit(solution)/shard_map/ppermute | solution.py:49
  98.0 34.5 %collective-permute-start.4 = (f32[20,1,64,256]{3,2,1,0:T(8,128)}, f32[20,1,64,256]{3,2,1,0:T(8,128)S(1)}, u32[]{:S(2)}, u32[]{:S(2)}) collective-permute-start(f32[20,1,64,256]{3,2,1,0:T(8,128)} %get-tuple-element.431), channel_id=1, source_target_pairs={{0,8},{8,16},{16,24},{24,32},{32,40},{40,48},{48,56},{56,64},{64,7... | collective-permute-start | bytes 3932168 | tf_op jit(solution)/shard_map/ppermute | solution.py:47
  134.0 7.3 %collective-permute-start.7 = (f32[20,6,1,256]{3,0,2,1:T(8,128)S(1)}, f32[20,6,1,256]{3,0,2,1:T(8,128)S(1)}, u32[]{:S(2)}, u32[]{:S(2)}) collective-permute-start(f32[20,6,1,256]{3,0,2,1:T(8,128)S(1)} %copy.141), channel_id=1, source_target_pairs={{1,0},{2,1},{3,2},{4,3},{5,4},{6,5},{7,6},{9,8},{10,9},{11,10},{12... | collective-permute-start | bytes 368648 | tf_op jit(solution)/shard_map/ppermute | solution.py:49
  135.3 6.1 collective-permute-start.6
  141.3 12.9 %slice-start = ((s8[5242880]{0:T(1024)(128)(4,1)}), s8[4194304]{0:T(1024)(128)(4,1)S(1)}, s32[]{:S(2)}) async-start(s8[5242880]{0:T(1024)(128)(4,1)} %bitcast.166), calls=%async_computation.2 | async-start | bytes 8388608
  142.6 11.6 %copy-start.11 = (f32[20,6,1,256]{3,2,1,0:T(1,128)}, f32[20,6,1,256]{3,2,1,0:T(1,128)S(1)}, u32[]{:S(2)}) copy-start(f32[20,6,1,256]{3,2,1,0:T(1,128)S(1)} %copy.140) | copy-start | bytes 368644
  142.6 11.6 %slice-start.1 = ((s8[5242880]{0:T(1024)(128)(4,1)}), s8[1048576]{0:T(1024)(128)(4,1)S(1)}, s32[]{:S(2)}) async-start(s8[5242880]{0:T(1024)(128)(4,1)} %bitcast.166), calls=%async_computation.3 | async-start | bytes 2097152
  162.7 17.0 %copy-start.2 = (f32[1,4,64,256]{3,2,1,0:T(8,128)S(1)}, f32[1,4,64,256]{3,2,1,0:T(8,128)}, u32[]{:S(2)}) copy-start(f32[1,4,64,256]{3,2,1,0:T(8,128)} %get-tuple-element.302) | copy-start | bytes 786436
  162.7 17.8 %copy-start.3 = (f32[1,4,64,256]{3,2,1,0:T(8,128)S(1)}, f32[1,4,64,256]{3,2,1,0:T(8,128)}, u32[]{:S(2)}) copy-start(f32[1,4,64,256]{3,2,1,0:T(8,128)} %get-tuple-element.303) | copy-start | bytes 786436
  162.7 17.8 %copy-start.4 = (f32[1,4,64,256]{3,2,1,0:T(8,128)S(1)}, f32[1,4,64,256]{3,2,1,0:T(8,128)}, u32[]{:S(2)}) copy-start(f32[1,4,64,256]{3,2,1,0:T(8,128)} %get-tuple-element.304) | copy-start | bytes 786436
  162.7 17.7 %copy-start.5 = (f32[1,4,64,256]{3,2,1,0:T(8,128)S(1)}, f32[1,4,64,256]{3,2,1,0:T(8,128)}, u32[]{:S(2)}) copy-start(f32[1,4,64,256]{3,2,1,0:T(8,128)} %get-tuple-element.305) | copy-start | bytes 786436
  162.7 17.7 %copy-start.6 = (f32[1,4,64,256]{3,2,1,0:T(8,128)S(1)}, f32[1,4,64,256]{3,2,1,0:T(8,128)}, u32[]{:S(2)}) copy-start(f32[1,4,64,256]{3,2,1,0:T(8,128)} %get-tuple-element.306) | copy-start | bytes 786436
  162.7 17.7 %copy-start.7 = (f32[1,4,64,256]{3,2,1,0:T(8,128)S(1)}, f32[1,4,64,256]{3,2,1,0:T(8,128)}, u32[]{:S(2)}) copy-start(f32[1,4,64,256]{3,2,1,0:T(8,128)} %get-tuple-element.307) | copy-start | bytes 786436
  162.7 17.7 %copy-start.8 = (f32[1,4,64,256]{3,2,1,0:T(8,128)S(1)}, f32[1,4,64,256]{3,2,1,0:T(8,128)}, u32[]{:S(2)}) copy-start(f32[1,4,64,256]{3,2,1,0:T(8,128)} %get-tuple-element.308) | copy-start | bytes 786436
  162.7 17.7 %copy-start.9 = (f32[1,4,64,256]{3,2,1,0:T(8,128)S(1)}, f32[1,4,64,256]{3,2,1,0:T(8,128)}, u32[]{:S(2)}) copy-start(f32[1,4,64,256]{3,2,1,0:T(8,128)} %get-tuple-element.309) | copy-start | bytes 786436
  162.8 17.7 %copy-start.10 = (f32[1,4,64,256]{3,2,1,0:T(8,128)S(1)}, f32[1,4,64,256]{3,2,1,0:T(8,128)}, u32[]{:S(2)}) copy-start(f32[1,4,64,256]{3,2,1,0:T(8,128)} %get-tuple-element.310) | copy-start | bytes 786436
  162.8 17.7 %copy-start.12 = (f32[1,4,64,256]{3,2,1,0:T(8,128)S(1)}, f32[1,4,64,256]{3,2,1,0:T(8,128)}, u32[]{:S(2)}) copy-start(f32[1,4,64,256]{3,2,1,0:T(8,128)} %get-tuple-element.294) | copy-start | bytes 786436
  162.8 17.7 %copy-start.13 = (f32[1,4,64,256]{3,2,1,0:T(8,128)S(1)}, f32[1,4,64,256]{3,2,1,0:T(8,128)}, u32[]{:S(2)}) copy-start(f32[1,4,64,256]{3,2,1,0:T(8,128)} %get-tuple-element.301) | copy-start | bytes 786436
  174.7 10.3 %copy-start.14 = (f32[1,4,64,256]{3,2,1,0:T(8,128)S(1)}, f32[1,4,64,256]{3,2,1,0:T(8,128)}, u32[]{:S(2)}) copy-start(f32[1,4,64,256]{3,2,1,0:T(8,128)} %get-tuple-element.293) | copy-start | bytes 786436
  186.0 52.2 %copy-start.32 = (f32[8,3,512]{2,1,0:T(4,128)S(1)}, f32[8,3,512]{2,1,0:T(4,128)}, u32[]{:S(2)}) copy-start(f32[8,3,512]{2,1,0:T(4,128)} %custom-call.11) | copy-start | bytes 147460
  225.1 13.1 %all-to-all-start = ((f32[8,1,3,512]{3,1,2,0:T(1,128)}), f32[8,1,3,512]{3,1,2,0:T(1,128)S(1)}, u32[]{:S(2)}, u32[]{:S(2)}) async-start(f32[8,1,3,512]{3,1,2,0:T(1,128)} %copy.147), calls=%async_computation | async-start | bytes 98304 | tf_op jit(solution)/shard_map/all_to_all | solution.py:172
  616.3 8.4 %all-to-all-start.1 = ((f32[8,1,3,512]{3,1,2,0:T(1,128)}), f32[8,1,3,512]{3,1,2,0:T(1,128)S(1)}, u32[]{:S(2)}, u32[]{:S(2)}) async-start(f32[8,1,3,512]{3,1,2,0:T(1,128)} %copy.153), calls=%async_computation.1 | async-start | bytes 98304 | tf_op jit(solution)/shard_map/all_to_all | solution.py:178
  (15 other events, 62.1 us)
where the time goes:
time: 700 us; the launch traced here: 693 us
  loops' own time  247 us (35%)
  other arithmetic  179 us (26%)
  local copies, waits for them, and re-layouts  163 us (23%)
  waiting for transfers between devices  74.6 us (11%)
  starting transfers between devices  28.5 us (4%)
    another operation x8, loops' own time, pair_forces(): total, unused = lax.scan(one_pair, start, (pair_list, noise))  246 us
    scatter-add x3, other arithmetic, per_device(): jax.ops.segment_sum(back[:, comp, :].reshape(-1), flat_ids, num_segments=...  66.6 us
    slice x64, local copies, waits for them, and re-layouts, one_pair(): pos_b = lax.dynamic_index_in_dim(pos_tiles, pair[1], 1, keepdims=False)  37.1 us
    unnamed x40, other arithmetic  36.8 us
    ppermute x4, waiting for transfers between devices, padded_2(): lax.ppermute(head, axis, [((i + 1) % count, i) for i in range(ends)])  34.9 us
    ppermute x4, waiting for transfers between devices, padded_2(): lax.ppermute(tail, axis, [(i, (i + 1) % count) for i in range(ends)])  30.9 us
    unnamed x96, local copies, waits for them, and re-layouts  25.9 us
    dynamic_update_slice x32, local copies, waits for them, and re-layouts, per_device(): lax.map(patch_step, (positions, velocities, received, pair_tiles, pair_no...  23.2 us
  transfers between devices with their start and end apart: 10, of which 7 were waited for; matrix products, arithmetic and copies ran while one was open for 1% of the time, Pallas kernels for 0%

commit v1 on v0

--- a/solution.py
+++ b/solution.py
@@ -1,6 +1,8 @@
 import jax
 import jax.numpy as jnp
 from jax import lax
+from jax.experimental import pallas as pl
+from jax.experimental.pallas import tpu as pltpu
 from jax.sharding import PartitionSpec as P
 
 LATTICE_DIRS = [
@@ -31,9 +33,12 @@
 REPULSION = 25.0
 FRICTION = 4.5
 NOISE_AMP = 3.0
+NOISE_SCALE = 15.0
 DRAG_COEFF = 12.5
 VELOCITY_SCALE = 20.0
 SOFTENING = 0.01
+BF16 = jnp.bfloat16
+F32 = jnp.float32
 
 
 def padded_2(cells, sides, width, closed):
@@ -113,44 +118,152 @@
     return stream_padded(pad_depth(full), post)
 
 
-def pair_forces(position, velocity, pair_list, noise):
-    tile = noise.shape[-1]
-    count = position.shape[1] // tile
-    pos_tiles = position.reshape(3, count, tile)
-    vel_tiles = velocity.reshape(3, count, tile)
-
-    def one_pair(carry, item):
-        pair, noise_tile = item
-        pos_a = lax.dynamic_index_in_dim(pos_tiles, pair[0], 1, keepdims=False)
-        pos_b = lax.dynamic_index_in_dim(pos_tiles, pair[1], 1, keepdims=False)
-        vel_a = lax.dynamic_index_in_dim(vel_tiles, pair[0], 1, keepdims=False)
-        vel_b = lax.dynamic_index_in_dim(vel_tiles, pair[1], 1, keepdims=False)
-        delta = pos_a[:, :, None] - pos_b[:, None, :]
-        distance = jnp.sqrt(jnp.sum(delta * delta, axis=0) + SOFTENING)
-        weight = jnp.maximum(0.0, 1.0 - distance)
-        unit = delta / distance
-        along = jnp.sum(unit * (vel_a[:, :, None] - vel_b[:, None, :]), axis=0)
-        scalar = (
-            REPULSION * weight
-            - FRICTION * weight * weight * along
-            + NOISE_AMP * weight * noise_tile.astype(jnp.float32) / jnp.sqrt(TIME_STEP)
+def pair_patch(g, tiles, pos, vel, noise, force, rows, cols, noise_t):
+    bead_tiles = rows.shape[0]
+    pairs = noise.shape[1]
+    tile = noise.shape[2]
+    for t in range(bead_tiles):
+        span = slice(t * tile, (t + 1) * tile)
+        rows[t, 0:3, :] = pos[g, :, span]
+        rows[t, 3:6, :] = vel[g, :, span]
+        turned = rows[t].T
+        for c in range(6):
+            cols[t, c] = jnp.broadcast_to(turned[:, c : c + 1], (tile, tile))
+    sub = lax.broadcasted_iota(jnp.int32, (tile, tile), 0)
+    lane = lax.broadcasted_iota(jnp.int32, (tile, tile), 1)
+    scaled_eye = jnp.where(sub == lane, NOISE_SCALE, 0.0).astype(BF16)
+    step = 32
+
+    def one_pair(p, carry):
+        first, second = tiles[g, p, 0], tiles[g, p, 1]
+        noise_t[...] = lax.dot_general(
+            scaled_eye, noise[g, p], (((1,), (1,)), ((), ())), preferred_element_type=F32
         )
-        force = jnp.sum(scalar[None] * unit, axis=2)
-        current = lax.dynamic_index_in_dim(carry, pair[0], 1, keepdims=False)
-        carry = lax.dynamic_update_index_in_dim(carry, current + force, pair[0], 1)
-        return (carry, None)
-
-    start = jnp.zeros((3, count, tile), jnp.float32)
-    total, unused = lax.scan(one_pair, start, (pair_list, noise))
-    return total.reshape(3, count * tile)
-
-
-def patch_step(item):
-    position, velocity, flow, pair_list, noise = item
-    drag = DRAG_COEFF * (flow - velocity)
-    new_vel = velocity + TIME_STEP * (pair_forces(position, velocity, pair_list, noise) + drag)
-    new_pos = position + TIME_STEP * new_vel
-    return (new_pos, new_vel, -TIME_STEP * drag)
+        own = rows[first]
+        own = [jnp.broadcast_to(own[c : c + 1, :], (step, tile)) for c in range(6)]
+        sums = [None] * 3
+        for start in range(0, tile, step):
+            part = slice(start, start + step)
+            gap = [own[c] - cols[second, c, part, :] for c in range(6)]
+            dist_sq = gap[0] * gap[0] + gap[1] * gap[1] + gap[2] * gap[2] + SOFTENING
+            inverse = lax.rsqrt(dist_sq)
+            weight = jnp.maximum(0.0, 1.0 - dist_sq * inverse)
+            over = weight * inverse
+            along = gap[0] * gap[3] + gap[1] * gap[4] + gap[2] * gap[5]
+            scalar = over * (REPULSION + noise_t[part, :] - FRICTION * (over * along))
+            for c in range(3):
+                piece = (scalar * gap[c]).reshape(step // 8, 8, tile).sum(axis=0)
+                sums[c] = piece if sums[c] is None else sums[c] + piece
+        out = []
+        for t in range(bead_tiles):
+            for c in range(3):
+                out.append(carry[t * 3 + c] + jnp.where(first == t, sums[c], 0.0))
+        return tuple(out)
+
+    zero = jnp.zeros((8, tile), F32)
+    total = lax.fori_loop(0, pairs, one_pair, (zero,) * (3 * bead_tiles))
+    for t in range(bead_tiles):
+        for c in range(3):
+            force[g, c : c + 1, t * tile : (t + 1) * tile] = total[t * 3 + c].sum(
+                axis=0, keepdims=True
+            )
+
+
+def pair_kernel(tiles, pos, vel, noise, force, rows, cols, noise_t):
+    lax.fori_loop(
+        0,
+        pos.shape[0],
+        lambda g, _: (pair_patch(g, tiles, pos, vel, noise, force, rows, cols, noise_t), 0)[1],
+        0,
+    )
+
+
+def pair_forces(pos, vel, tiles, noise):
+    tile = noise.shape[2]
+    count = pos.shape[2] // tile
+    vmem = pl.BlockSpec(memory_space=pltpu.VMEM)
+    return pl.pallas_call(
+        pair_kernel,
+        out_shape=jax.ShapeDtypeStruct(pos.shape, F32),
+        in_specs=[pl.BlockSpec(memory_space=pltpu.SMEM), vmem, vmem, vmem],
+        out_specs=vmem,
+        scratch_shapes=[
+            pltpu.VMEM((count, 8, tile), F32),
+            pltpu.VMEM((count, 6, tile, tile), F32),
+            pltpu.VMEM((tile, tile), F32),
+        ],
+        compiler_params=pltpu.CompilerParams(vmem_limit_bytes=32 * 2**20),
+    )(tiles, pos, vel, noise)
+
+
+def two_parts(value):
+    high = value.astype(BF16)
+    return high, (value - high.astype(F32)).astype(BF16)
+
+
+def one_hot(index, size):
+    beads = index.shape[1]
+    rows = lax.broadcasted_iota(jnp.int32, (size, beads), 0)
+    return jnp.where(rows == index, 1.0, 0.0).astype(BF16)
+
+
+def gather_kernel(table, voxel, flow):
+    depth = table.shape[2]
+    lines = table.shape[1]
+    parts = [two_parts(table[c]) for c in range(3)]
+
+    def one_patch(g, _):
+        index = voxel[pl.ds(g, 1), :]
+        low, high = lax.rem(index, depth), lax.div(index, depth)
+        hot = one_hot(low, depth)
+        beads = index.shape[1]
+        hit = lax.broadcasted_iota(jnp.int32, (lines, beads), 0) == high
+        for c in range(3):
+            got = jnp.dot(parts[c][0], hot, preferred_element_type=F32) + jnp.dot(
+                parts[c][1], hot, preferred_element_type=F32
+            )
+            flow[g, c : c + 1, :] = VELOCITY_SCALE * jnp.where(hit, got, 0.0).sum(
+                axis=0, keepdims=True
+            )
+        return 0
+
+    lax.fori_loop(0, voxel.shape[0], one_patch, 0)
+
+
+def scatter_kernel(reaction, voxel, field):
+    lines, depth = field.shape[1], field.shape[2]
+    field[...] = jnp.zeros_like(field)
+
+    def one_patch(g, _):
+        index = voxel[pl.ds(g, 1), :]
+        low, high = lax.rem(index, depth), lax.div(index, depth)
+        hot_low = one_hot(low, depth)
+        hot_high = one_hot(high, lines)
+        for c in range(3):
+            line = jnp.broadcast_to(reaction[g, c : c + 1, :], (lines, index.shape[1]))
+            total = field[c]
+            for part in two_parts(line):
+                total = total + lax.dot_general(
+                    hot_high * part,
+                    hot_low,
+                    (((1,), (1,)), ((), ())),
+                    preferred_element_type=F32,
+                )
+            field[c] = total
+        return 0
+
+    lax.fori_loop(0, voxel.shape[0], one_patch, 0)
+
+
+def vmem_call(kernel, out_shape, *args):
+    vmem = pl.BlockSpec(memory_space=pltpu.VMEM)
+    return pl.pallas_call(
+        kernel,
+        out_shape=jax.ShapeDtypeStruct(out_shape, F32),
+        in_specs=[vmem] * len(args),
+        out_specs=vmem,
+        compiler_params=pltpu.CompilerParams(vmem_limit_bytes=32 * 2**20),
+    )(*args)
 
 
 def per_device(
@@ -161,20 +274,22 @@
     for step in range(2):
         dist = lattice_step(dist, fluid)
     density, comps = moments(dist)
-    cells = dist.shape[1] * dist.shape[2] * dist.shape[3]
-    velocity_flat = VELOCITY_SCALE * jnp.stack(comps).reshape(3, cells)
+    size_x, size_y, size_z = dist.shape[1:]
+    table = jnp.stack(comps).reshape(3, size_x * size_y, size_z)
     patch_count, bead_count = patch_voxel.shape
     owners = lax.axis_size("xs")
     share = patch_count // owners
-    at_beads = jnp.transpose(velocity_flat[:, patch_voxel], (1, 0, 2))
+    pair = pair_forces(positions, velocities, pair_tiles, pair_noise)
+    at_beads = vmem_call(gather_kernel, (patch_count, 3, bead_count), table, patch_voxel)
     order = jnp.argsort(patch_owner, stable=True)
     grouped = at_beads[order].reshape(owners, share, 3, bead_count)
     received = lax.all_to_all(grouped, "xs", split_axis=0, concat_axis=0, tiled=True).reshape(
         patch_count, 3, bead_count
     )
-    new_pos, new_vel, reaction = lax.map(
-        patch_step, (positions, velocities, received, pair_tiles, pair_noise)
-    )
+    drag = DRAG_COEFF * (received - velocities)
+    new_vel = velocities + TIME_STEP * (pair + drag)
+    new_pos = positions + TIME_STEP * new_vel
+    reaction = -TIME_STEP * drag
     returned = lax.all_to_all(
         reaction.reshape(owners, share, 3, bead_count),
         "xs",
@@ -184,14 +299,8 @@
     )
     returned = returned.reshape(patch_count, 3, bead_count)
     back = returned[jnp.argsort(order)]
-    flat_ids = patch_voxel.reshape(-1)
-    field = jnp.stack(
-        [
-            jax.ops.segment_sum(back[:, comp, :].reshape(-1), flat_ids, num_segments=cells)
-            for comp in range(3)
-        ]
-    )
-    return (dist, new_pos, new_vel, field.reshape(3, dist.shape[1], dist.shape[2], dist.shape[3]))
+    field = vmem_call(scatter_kernel, (3, size_x * size_y, size_z), back, patch_voxel)
+    return (dist, new_pos, new_vel, field.reshape(3, size_x, size_y, size_z))
 
 
 def solution(mesh):

time: 700 us -> 232 us (0.33)
  loops' own time: 247 us -> 0 us
  local copies, waits for them, and re-layouts: 163 us -> 32.2 us
  other arithmetic: 179 us -> 72.9 us
  Pallas kernels: 0 us -> 29.2 us
  waiting for transfers between devices: 74.6 us -> 66.9 us
    another operation x9 -> x0, loops' own time: 247 us -> none  [the longest x8 246 us: pair_forces(): total, unused = lax.scan(one_pair, start, (pair_list, noise))]
    scatter-add x3 -> x0, other arithmetic: 66.6 us -> none  [per_device(): jax.ops.segment_sum(back[:, comp, :].reshape(-1), flat_ids, num_segments=...]
    slice x65 -> x0, local copies, waits for them, and re-layouts: 37.2 us -> none  [the longest x64 37.1 us: one_pair(): pos_b = lax.dynamic_index_in_dim(pos_tiles, pair[1], 1, keepdims=False)]
    reduce_sum x192 -> x0, other arithmetic: 32.6 us -> none  [the longest x64 14.5 us: one_pair(): force = jnp.sum(scalar[None] * unit, axis=2)]
    pallas_call x0 -> x3, Pallas kernels: none -> 29.2 us  [the longest x1 17.9 us: pair_forces(): pl.pallas_call(pair_kernel, out_shape=jax.ShapeDtypeStruct(pos.shape, F32...]
    ppermute x4, waiting for transfers between devices: 34.9 us -> 5.79 us  [padded_2(): lax.ppermute(head, axis, [((i + 1) % count, i) for i in range(ends)])]
    ppermute x4, waiting for transfers between devices: 30.9 us -> 56.4 us  [padded_2(): lax.ppermute(tail, axis, [(i, (i + 1) % count) for i in range(ends)])]
    dynamic_update_slice x32 -> x0, local copies, waits for them, and re-layouts: 23.2 us -> none  [per_device(): lax.map(patch_step, (positions, velocities, received, pair_tiles, pair_no...]
  transfers between devices with their start and end apart: 10 -> 10, of which waited for: 7 -> 7; matrix products, arithmetic and copies ran while one was open for 1% -> 5% of each run, Pallas kernels for 0% -> 8%
where the time goes in v1:
time: 232 us; the launch traced here: 228 us
  other arithmetic  72.9 us (31%)
  waiting for transfers between devices  66.9 us (29%)
  local copies, waits for them, and re-layouts  32.2 us (14%)
  Pallas kernels  29.2 us (13%)
  starting transfers between devices  26.1 us (11%)
    ppermute x4, waiting for transfers between devices, padded_2(): lax.ppermute(tail, axis, [(i, (i + 1) % count) for i in range(ends)])  56.4 us
    unnamed x39, other arithmetic  36.2 us
    unnamed x102, local copies, waits for them, and re-layouts  23.1 us
    concatenate x3, other arithmetic, padded_2(): jnp.concatenate([lax.ppermute(tail, axis, [(i, (i + 1) % count) for i in...  20.5 us
    pallas_call x1, Pallas kernels, pair_forces(): pl.pallas_call(pair_kernel, out_shape=jax.ShapeDtypeStruct(pos.shape, F32...  17.9 us
    ppermute x4, starting transfers between devices, padded_2(): lax.ppermute(tail, axis, [(i, (i + 1) % count) for i in range(ends)])  12.4 us
    pallas_call x2, Pallas kernels, vmem_call(): pl.pallas_call(kernel, out_shape=jax.ShapeDtypeStruct(out_shape, F32), in...  11.3 us
    div x2, other arithmetic, moments(): comps.append(total / density)  9.16 us
  transfers between devices with their start and end apart: 10, of which 7 were waited for; matrix products, arithmetic and copies ran while one was open for 5% of the time, Pallas kernels for 8%

profile of v1, /device:TPU:1, one launch (start us, length us, event | category | flops | bytes accessed | tf_op | source)
XLA Modules:
  0.0 228.5 jit_solution(12799960627541440112)
XLA Ops:
  0.6 2.8 %reduce_sum.2287 = f32[4,64,256]{2,1,0:T(8,128)S(1)} reduce(f32[19,4,64,256]{3,2,1,0:T(8,128)} %param.8, f32[]{:T(128)} %constant.58.clone.1), dimensions={0}, to_apply=%region_0.0 | reduce | flops 1179648 | bytes 5242884 | tf_op jit(solution)/shard_map/reduce_sum | solution.py:62
  3.4 3.8 %constant_dynamic-update-slice_fusion.18 = (f32[20,4,64,256]{3,2,1,0:T(8,128)S(1)}, f32[1,4,64,256]{3,2,1,0:T(8,128)}, f32[1,4,64,256]{3,2,1,0:T(8,128)S(1)}, f3...) fusion(f32[4,64,256]{2,1,0:T(8,128)S(1)} %reduce_sum.2287, ...), kind=kLoop, calls=%fused_computation.421 | loop fusion | flops 4194303 | bytes 6815744
  16.5 5.1 %collective-permute-start = (f32[20,1,64,256]{3,2,1,0:T(8,128)S(1)}, f32[20,1,64,256]{3,2,1,0:T(8,128)S(1)}, u32[]{:S(2)}, u32[]{:S(2)}) collective-permute-start(f32[20,1,64,256]{3,2,1,0:T(8,128)S(1)} %get-tuple-element.156), channel_id=1, source_target_pairs={{0,8},{8,16},{16,24},{24,32},{32,40},{40,48},{48,56},{56,64},{64,7... | collective-permute-start | bytes 3932168 | tf_op jit(solution)/shard_map/ppermute | solution.py:52
  21.5 30.2 %collective-permute-done = f32[20,1,64,256]{3,2,1,0:T(8,128)S(1)} collective-permute-done((f32[20,1,64,256]{3,2,1,0:T(8,128)S(1)}, f32[20,1,64,256]{3,2,1,0:T(8,128)S(1)}, u32[]{:S(2)}, u32[]{:S(2)}) %collective-permute-start) | collective-permute-done | bytes 1310752 | tf_op jit(solution)/shard_map/ppermute | solution.py:52
  51.7 2.1 collective-permute-done.1
  57.8 3.7 %collective-permute-done.3 = f32[20,6,1,256]{3,0,2,1:T(8,128)S(1)} collective-permute-done((f32[20,6,1,256]{3,0,2,1:T(8,128)S(1)}, f32[20,6,1,256]{3,0,2,1:T(8,128)S(1)}, u32[]{:S(2)}, u32[]{:S(2)}) %collective-permute-start.3) | collective-permute-done | bytes 122912 | tf_op jit(solution)/shard_map/ppermute | solution.py:54
  61.7 8.1 %select_maximum_fusion.4 = f32[20,6,66,258]{3,2,1,0:T(8,128)S(1)} fusion(f32[20,6,1,256]{3,2,1,0:T(1,128)S(1)} %copy.78, f32[20,6,1,256]{3,2,1,0:T(1,128)S(1)} %copy.76, f32[20,1,64,256]{3,2,1,0:T(8,128)S(1)} %collective-permute-done.1, f32[20,4,64,256]{3,2,1,0:T(8,128)S(1)} %bitcast_dynamic-update-slice_fusion.1, f32[20,1,64,256]{3,2,1,0:T(8,128)S(1)} %collective-permute-done), kind=kLoop, calls=%fused_computation.8 | loop fusion | flops 24520320 | bytes 16283520 | tf_op jit(solution)/shard_map/concatenate | solution.py:50
  69.8 5.3 %constant_dynamic-update-slice_fusion.37 = (f32[20,4,64,256]{3,2,1,0:T(8,128)S(1)}, f32[1,4,64,256]{3,2,1,0:T(8,128)}, f32[1,4,64,256]{3,2,1,0:T(8,128)S(1)}, f3...) fusion(f32[1,4,64,256]{3,2,1,0:T(8,128)} %get-tuple-element.144, ...), kind=kLoop, calls=%fused_computation.440 | loop fusion | flops 10354687 | bytes 24887296
  75.1 1.9 constant_dynamic-update-slice_fusion.36
  76.9 1.8 constant_dynamic-update-slice_fusion.35
  78.8 1.8 constant_dynamic-update-slice_fusion.34
  93.4 2.3 copy-done.2
  95.7 1.7 fusion.283
  97.4 3.4 %collective-permute-start.4 = (f32[20,1,64,256]{3,2,1,0:T(8,128)}, f32[20,1,64,256]{3,2,1,0:T(8,128)S(1)}, u32[]{:S(2)}, u32[]{:S(2)}) collective-permute-start(f32[20,1,64,256]{3,2,1,0:T(8,128)} %get-tuple-element.153), channel_id=1, source_target_pairs={{0,8},{8,16},{16,24},{24,32},{32,40},{40,48},{48,56},{56,64},{64,7... | collective-permute-start | bytes 3932168 | tf_op jit(solution)/shard_map/ppermute | solution.py:52
  102.8 25.4 %collective-permute-done.4 = f32[20,1,64,256]{3,2,1,0:T(8,128)S(1)} collective-permute-done((f32[20,1,64,256]{3,2,1,0:T(8,128)}, f32[20,1,64,256]{3,2,1,0:T(8,128)S(1)}, u32[]{:S(2)}, u32[]{:S(2)}) %collective-permute-start.4) | collective-permute-done | bytes 1310752 | tf_op jit(solution)/shard_map/ppermute | solution.py:52
  128.2 2.1 pad_maximum_fusion.19
  131.0 2.3 collective-permute-start.6
  135.5 17.9 %shard_map.111 = f32[8,3,512]{2,1,0:T(4,128)S(1)} custom-call(s32[8,8,2]{2,1,0:T(8,128)S(1)} %copy.87.tiles, f32[8,3,512]{2,1,0:T(4,128)S(1)} %copy.95.pos, f32[8,3,512]{2,1,0:T(4,128)S(1)} %copy.94.vel, bf16[8,8,128,128]{3,2,1,0:T(8,128)(2,1)S(1)} %copy-done), custom_call_target="tpu_custom_call" | custom-call | tf_op jit(solution)/shard_map/pallas_call | solution.py:185
  153.4 1.7 constant_dynamic-update-slice_fusion.56
  157.6 12.2 %select_maximum_fusion = f32[20,6,66,258]{3,2,1,0:T(8,128)} fusion(f32[20,6,1,256]{3,2,1,0:T(1,128)S(1)} %copy.84, f32[20,6,1,256]{3,2,1,0:T(1,128)S(1)} %copy.82, f32[20,1,64,256]{3,2,1,0:T(8,128)} %collective-permute-done.5, f32[20,4,64,256]{3,2,1,0:T(8,128)} %copy-done.2, f32[20,1,64,256]{3,2,1,0:T(8,128)} %copy-done.4), kind=kLoop, calls=%fused_computation.4 | loop fusion | flops 24520320 | bytes 16283520 | tf_op jit(solution)/shard_map/concatenate | solution.py:50
  169.8 8.1 %add_divide_fusion.2 = (f32[1,4,64,256]{3,2,1,0:T(8,128)}, f32[1,4,64,256]{3,2,1,0:T(8,128)}, f32[1,4,64,256]{3,2,1,0:T(8,128)S(1)}, f32[1,4,64,256]{3,2,1,0:T(8...) fusion(f32[1,4,64,256]{3,2,1,0:T(8,128)S(1)} %copy-done.6, ...), kind=kLoop, calls=%fused_computation.379 | loop fusion | flops 7143424 | bytes 23576576 | tf_op jit(solution)/shard_map/div | solution.py:70
  178.0 1.8 constant_dynamic-update-slice_fusion.55
  179.8 1.7 constant_dynamic-update-slice_fusion.54
  181.5 1.7 constant_dynamic-update-slice_fusion.53
  183.2 1.7 constant_dynamic-update-slice_fusion.52
  184.9 1.7 constant_dynamic-update-slice_fusion.51
  186.5 1.7 constant_dynamic-update-slice_fusion.50
  193.0 5.3 %shard_map.112 = f32[8,3,512]{2,1,0:T(4,128)S(1)} custom-call(f32[3,256,256]{2,1,0:T(8,128)S(1)} %pad_maximum_fusion.table, s32[8,512]{1,0:T(8,128)S(1)} %copy-done.1), custom_call_target="tpu_custom_call" | custom-call | tf_op jit(solution)/shard_map/pallas_call | solution.py:260
  199.5 7.6 %all-to-all-start = ((f32[8,1,3,512]{3,1,2,0:T(1,128)}), f32[8,1,3,512]{3,1,2,0:T(1,128)S(1)}, u32[]{:S(2)}, u32[]{:S(2)}) async-start(f32[8,1,3,512]{3,1,2,0:T(1,128)} %copy.90), calls=%async_computation | async-start | bytes 98304 | tf_op jit(solution)/shard_map/all_to_all | solution.py:286
  213.1 3.6 %all-to-all-start.1 = ((f32[8,1,3,512]{3,1,2,0:T(1,128)}), f32[8,1,3,512]{3,1,2,0:T(1,128)S(1)}, u32[]{:S(2)}, u32[]{:S(2)}) async-start(f32[8,1,3,512]{3,1,2,0:T(1,128)} %copy.96), calls=%async_computation.1 | async-start | bytes 98304 | tf_op jit(solution)/shard_map/all_to_all | solution.py:293
  218.7 3.2 %all-to-all-done.1 = f32[8,1,3,512]{3,1,2,0:T(1,128)S(1)} async-done(((f32[8,1,3,512]{3,1,2,0:T(1,128)}), f32[8,1,3,512]{3,1,2,0:T(1,128)S(1)}, u32[]{:S(2)}, u32[]{:S(2)}) %all-to-all-start.1) | async-done | bytes 49184 | tf_op jit(solution)/shard_map/all_to_all | solution.py:293
  222.5 6.0 %shard_map.113 = f32[3,256,256]{2,1,0:T(8,128)} custom-call(f32[8,3,512]{2,1,0:T(4,128)S(1)} %gather_fusion.1, s32[8,512]{1,0:T(8,128)S(1)} %copy-done.1), custom_call_target="tpu_custom_call" | custom-call | tf_op jit(solution)/shard_map/pallas_call | solution.py:260
  (169 shorter events, 47.9 us)
Async XLA Ops:
  16.5 35.2 %collective-permute-start = (f32[20,1,64,256]{3,2,1,0:T(8,128)S(1)}, f32[20,1,64,256]{3,2,1,0:T(8,128)S(1)}, u32[]{:S(2)}, u32[]{:S(2)}) collective-permute-start(f32[20,1,64,256]{3,2,1,0:T(8,128)S(1)} %get-tuple-element.156), channel_id=1, source_target_pairs={{0,8},{8,16},{16,24},{24,32},{32,40},{40,48},{48,56},{56,64},{64,7... | collective-permute-start | bytes 3932168 | tf_op jit(solution)/shard_map/ppermute | solution.py:52
  21.5 32.3 %collective-permute-start.1 = (f32[20,1,64,256]{3,2,1,0:T(8,128)S(1)}, f32[20,1,64,256]{3,2,1,0:T(8,128)S(1)}, u32[]{:S(2)}, u32[]{:S(2)}) collective-permute-start(f32[20,1,64,256]{3,2,1,0:T(8,128)S(1)} %get-tuple-element.155), channel_id=1, source_target_pairs={{8,0},{16,8},{24,16},{32,24},{40,32},{48,40},{56,48},{64,56},{72,6... | collective-permute-start | bytes 3932168 | tf_op jit(solution)/shard_map/ppermute | solution.py:54
  54.0 3.7 %collective-permute-start.2 = (f32[20,6,1,256]{3,0,2,1:T(8,128)S(1)}, f32[20,6,1,256]{3,0,2,1:T(8,128)S(1)}, u32[]{:S(2)}, u32[]{:S(2)}) collective-permute-start(f32[20,6,1,256]{3,0,2,1:T(8,128)S(1)} %copy.75), channel_id=1, source_target_pairs={{0,1},{1,2},{2,3},{3,4},{4,5},{5,6},{6,7},{8,9},{9,10},{10,11},{11... | collective-permute-start | bytes 368648 | tf_op jit(solution)/shard_map/ppermute | solution.py:52
  55.6 5.9 %collective-permute-start.3 = (f32[20,6,1,256]{3,0,2,1:T(8,128)S(1)}, f32[20,6,1,256]{3,0,2,1:T(8,128)S(1)}, u32[]{:S(2)}, u32[]{:S(2)}) collective-permute-start(f32[20,6,1,256]{3,0,2,1:T(8,128)S(1)} %copy.77), channel_id=1, source_target_pairs={{1,0},{2,1},{3,2},{4,3},{5,4},{6,5},{7,6},{9,8},{10,9},{11,10},{12... | collective-permute-start | bytes 368648 | tf_op jit(solution)/shard_map/ppermute | solution.py:54
  75.0 7.3 %copy-start.28 = (f32[1,4,64,256]{3,2,1,0:T(8,128)S(1)}, f32[1,4,64,256]{3,2,1,0:T(8,128)}, u32[]{:S(2)}) copy-start(f32[1,4,64,256]{3,2,1,0:T(8,128)} %get-tuple-element.94) | copy-start | bytes 786436
  91.7 9.1 %copy-start.37 = (s32[8]{0:T(128)S(1)}, s32[8]{0:T(128)}, u32[]{:S(2)}) copy-start(s32[8]{0:T(128)} %param.11) | copy-start | bytes 100
  97.4 37.9 %copy-start.34 = (f32[8,3,512]{2,0,1:T(8,128)S(1)}, f32[8,3,512]{2,0,1:T(8,128)}, u32[]{:S(2)}) copy-start(f32[8,3,512]{2,0,1:T(8,128)} %param.13) | copy-start | bytes 147460
  97.4 37.9 %copy-start.33 = (f32[8,3,512]{2,0,1:T(8,128)S(1)}, f32[8,3,512]{2,0,1:T(8,128)}, u32[]{:S(2)}) copy-start(f32[8,3,512]{2,0,1:T(8,128)} %param.12) | copy-start | bytes 147460
  97.4 38.0 %copy-start.36 = (s32[8,8,2]{1,2,0:T(2,128)S(1)}, s32[8,8,2]{1,2,0:T(2,128)}, u32[]{:S(2)}) copy-start(s32[8,8,2]{1,2,0:T(2,128)} %param.14) | copy-start | bytes 1540
  97.4 38.1 %copy-start = (bf16[8,8,128,128]{3,2,1,0:T(8,128)(2,1)S(1)}, bf16[8,8,128,128]{3,2,1,0:T(8,128)(2,1)}, u32[]{:S(2)}) copy-start(bf16[8,8,128,128]{3,2,1,0:T(8,128)(2,1)} %noise.1) | copy-start | bytes 6291460
  97.4 30.8 %collective-permute-start.4 = (f32[20,1,64,256]{3,2,1,0:T(8,128)}, f32[20,1,64,256]{3,2,1,0:T(8,128)S(1)}, u32[]{:S(2)}, u32[]{:S(2)}) collective-permute-start(f32[20,1,64,256]{3,2,1,0:T(8,128)} %get-tuple-element.153), channel_id=1, source_target_pairs={{0,8},{8,16},{16,24},{24,32},{32,40},{40,48},{48,56},{56,64},{64,7... | collective-permute-start | bytes 3932168 | tf_op jit(solution)/shard_map/ppermute | solution.py:52
  100.8 27.4 %collective-permute-start.5 = (f32[20,1,64,256]{3,2,1,0:T(8,128)}, f32[20,1,64,256]{3,2,1,0:T(8,128)}, u32[]{:S(2)}, u32[]{:S(2)}) collective-permute-start(f32[20,1,64,256]{3,2,1,0:T(8,128)} %get-tuple-element.154), channel_id=1, source_target_pairs={{8,0},{16,8},{24,16},{32,24},{40,32},{48,40},{56,48},{64,56},{72,6... | collective-permute-start | bytes 3932168 | tf_op jit(solution)/shard_map/ppermute | solution.py:54
  128.2 7.0 %copy-start.4 = (f32[20,1,64,256]{3,2,1,0:T(8,128)}, f32[20,1,64,256]{3,2,1,0:T(8,128)S(1)}, u32[]{:S(2)}) copy-start(f32[20,1,64,256]{3,2,1,0:T(8,128)S(1)} %collective-permute-done.4) | copy-start | bytes 3932164
  131.0 24.1 %collective-permute-start.6 = (f32[20,6,1,256]{3,0,2,1:T(8,128)}, f32[20,6,1,256]{3,0,2,1:T(8,128)}, u32[]{:S(2)}, u32[]{:S(2)}) collective-permute-start(f32[20,6,1,256]{3,0,2,1:T(8,128)} %copy.81), channel_id=1, source_target_pairs={{0,1},{1,2},{2,3},{3,4},{4,5},{5,6},{6,7},{8,9},{9,10},{10,11},{11... | collective-permute-start | bytes 368648 | tf_op jit(solution)/shard_map/ppermute | solution.py:52
  133.9 22.4 %collective-permute-start.7 = (f32[20,6,1,256]{3,0,2,1:T(8,128)}, f32[20,6,1,256]{3,0,2,1:T(8,128)}, u32[]{:S(2)}, u32[]{:S(2)}) collective-permute-start(f32[20,6,1,256]{3,0,2,1:T(8,128)} %copy.83), channel_id=1, source_target_pairs={{1,0},{2,1},{3,2},{4,3},{5,4},{6,5},{7,6},{9,8},{10,9},{11,10},{12... | collective-permute-start | bytes 368648 | tf_op jit(solution)/shard_map/ppermute | solution.py:54
  155.1 14.7 %slice-start = ((s8[5242880]{0:T(1024)(128)(4,1)}), s8[4194304]{0:T(1024)(128)(4,1)S(1)}, s32[]{:S(2)}) async-start(s8[5242880]{0:T(1024)(128)(4,1)} %bitcast.83), calls=%async_computation.2 | async-start | bytes 8388608
  156.3 13.5 %copy-start.11 = (f32[20,6,1,256]{3,2,1,0:T(1,128)}, f32[20,6,1,256]{3,2,1,0:T(1,128)S(1)}, u32[]{:S(2)}) copy-start(f32[20,6,1,256]{3,2,1,0:T(1,128)S(1)} %copy.82) | copy-start | bytes 368644
  157.5 12.2 %copy-start.12 = (f32[20,6,1,256]{3,2,1,0:T(1,128)}, f32[20,6,1,256]{3,2,1,0:T(1,128)S(1)}, u32[]{:S(2)}) copy-start(f32[20,6,1,256]{3,2,1,0:T(1,128)S(1)} %copy.84) | copy-start | bytes 368644
  157.5 12.2 %slice-start.1 = ((s8[5242880]{0:T(1024)(128)(4,1)}), s8[1048576]{0:T(1024)(128)(4,1)S(1)}, s32[]{:S(2)}) async-start(s8[5242880]{0:T(1024)(128)(4,1)} %bitcast.83), calls=%async_computation.3 | async-start | bytes 2097152
  157.5 12.2 %copy-start.5 = (f32[20,1,64,256]{3,2,1,0:T(8,128)S(1)}, f32[20,1,64,256]{3,2,1,0:T(8,128)}, u32[]{:S(2)}) copy-start(f32[20,1,64,256]{3,2,1,0:T(8,128)} %copy-done.4) | copy-start | bytes 3932164
  157.5 12.2 %copy-start.6 = (f32[1,4,64,256]{3,2,1,0:T(8,128)S(1)}, f32[1,4,64,256]{3,2,1,0:T(8,128)}, u32[]{:S(2)}) copy-start(f32[1,4,64,256]{3,2,1,0:T(8,128)} %get-tuple-element.83) | copy-start | bytes 786436
  177.9 13.9 %copy-start.7 = (f32[1,4,64,256]{3,2,1,0:T(8,128)S(1)}, f32[1,4,64,256]{3,2,1,0:T(8,128)}, u32[]{:S(2)}) copy-start(f32[1,4,64,256]{3,2,1,0:T(8,128)} %get-tuple-element.40) | copy-start | bytes 786436
  177.9 13.9 %copy-start.8 = (f32[1,4,64,256]{3,2,1,0:T(8,128)S(1)}, f32[1,4,64,256]{3,2,1,0:T(8,128)}, u32[]{:S(2)}) copy-start(f32[1,4,64,256]{3,2,1,0:T(8,128)} %get-tuple-element.41) | copy-start | bytes 786436
  178.0 13.9 %copy-start.9 = (f32[1,4,64,256]{3,2,1,0:T(8,128)S(1)}, f32[1,4,64,256]{3,2,1,0:T(8,128)}, u32[]{:S(2)}) copy-start(f32[1,4,64,256]{3,2,1,0:T(8,128)} %get-tuple-element.42) | copy-start | bytes 786436
  178.0 13.9 %copy-start.10 = (f32[1,4,64,256]{3,2,1,0:T(8,128)S(1)}, f32[1,4,64,256]{3,2,1,0:T(8,128)}, u32[]{:S(2)}) copy-start(f32[1,4,64,256]{3,2,1,0:T(8,128)} %get-tuple-element.43) | copy-start | bytes 786436
  178.0 13.9 %copy-start.13 = (f32[1,4,64,256]{3,2,1,0:T(8,128)S(1)}, f32[1,4,64,256]{3,2,1,0:T(8,128)}, u32[]{:S(2)}) copy-start(f32[1,4,64,256]{3,2,1,0:T(8,128)} %get-tuple-element.27) | copy-start | bytes 786436
  178.0 13.9 %copy-start.14 = (f32[1,4,64,256]{3,2,1,0:T(8,128)S(1)}, f32[1,4,64,256]{3,2,1,0:T(8,128)}, u32[]{:S(2)}) copy-start(f32[1,4,64,256]{3,2,1,0:T(8,128)} %get-tuple-element.34) | copy-start | bytes 786436
  179.8 13.1 %copy-start.15 = (f32[1,4,64,256]{3,2,1,0:T(8,128)S(1)}, f32[1,4,64,256]{3,2,1,0:T(8,128)}, u32[]{:S(2)}) copy-start(f32[1,4,64,256]{3,2,1,0:T(8,128)} %get-tuple-element.26) | copy-start | bytes 786436
  184.8 8.1 %copy-start.1 = (s32[8,512]{1,0:T(8,128)S(1)}, s32[8,512]{1,0:T(8,128)}, u32[]{:S(2)}) copy-start(s32[8,512]{1,0:T(8,128)} %voxel.3) | copy-start | bytes 49156
  191.9 20.4 %copy-start.35 = (f32[8,3,512]{2,0,1:T(8,128)S(1)}, f32[8,3,512]{2,0,1:T(8,128)}, u32[]{:S(2)}) copy-start(f32[8,3,512]{2,0,1:T(8,128)} %param.13) | copy-start | bytes 147460
  199.5 12.7 %all-to-all-start = ((f32[8,1,3,512]{3,1,2,0:T(1,128)}), f32[8,1,3,512]{3,1,2,0:T(1,128)S(1)}, u32[]{:S(2)}, u32[]{:S(2)}) async-start(f32[8,1,3,512]{3,1,2,0:T(1,128)} %copy.90), calls=%async_computation | async-start | bytes 98304 | tf_op jit(solution)/shard_map/all_to_all | solution.py:286
  213.1 8.8 %all-to-all-start.1 = ((f32[8,1,3,512]{3,1,2,0:T(1,128)}), f32[8,1,3,512]{3,1,2,0:T(1,128)S(1)}, u32[]{:S(2)}, u32[]{:S(2)}) async-start(f32[8,1,3,512]{3,1,2,0:T(1,128)} %copy.96), calls=%async_computation.1 | async-start | bytes 98304 | tf_op jit(solution)/shard_map/all_to_all | solution.py:293
  (18 other events, 80.9 us)

commit v2 on v1

v2 whole, which is shorter than its diff:
```python
import jax
import jax.numpy as jnp
from jax import lax
from jax.experimental import pallas as pl
from jax.experimental.pallas import tpu as pltpu
from jax.sharding import PartitionSpec as P

LATTICE_DIRS = [
    (0, 0, 0),
    (1, 0, 0),
    (-1, 0, 0),
    (0, 1, 0),
    (0, -1, 0),
    (0, 0, 1),
    (0, 0, -1),
    (1, 1, 0),
    (-1, -1, 0),
    (1, -1, 0),
    (-1, 1, 0),
    (1, 0, 1),
    (-1, 0, -1),
    (1, 0, -1),
    (-1, 0, 1),
    (0, 1, 1),
    (0, -1, -1),
    (0, 1, -1),
    (0, -1, 1),
]
LATTICE_WEIGHTS = [1.0 / 3.0] + [1.0 / 18.0] * 6 + [1.0 / 36.0] * 12
OPPOSITE_DIR = [0, 2, 1, 4, 3, 6, 5, 8, 7, 10, 9, 12, 11, 14, 13, 16, 15, 18, 17]
ORDER = [k for sign in (-1, 0, 1) for k in range(19) if LATTICE_DIRS[k][0] == sign]
SLOT = [ORDER.index(k) for k in range(19)]
PLUS_Y = [k for k in range(19) if LATTICE_DIRS[k][1] == 1]
MINUS_Y = [k for k in range(19) if LATTICE_DIRS[k][1] == -1]
CORNERS = [7, 8, 9, 10]
RELAX_TIME = 0.8
TIME_STEP = 0.04
REPULSION = 25.0
FRICTION = 4.5
NOISE_AMP = 3.0
NOISE_SCALE = 15.0
DRAG_COEFF = 12.5
VELOCITY_SCALE = 20.0
SOFTENING = 0.01
BF16 = jnp.bfloat16
F32 = jnp.float32
MESH = pl.DeviceIdType.MESH
PAD = 8


def moments(dist):
    density = dist[0]
    gaps = {}
    for k in range(1, 19, 2):
        density = density + (dist[k] + dist[k + 1])
        gaps[k] = dist[k] - dist[k + 1]
    inverse = 1.0 / density
    comps = []
    for axis in range(3):
        total = None
        for k in range(1, 19, 2):
            sign = LATTICE_DIRS[k][axis]
            if sign == 0:
                continue
            if total is None:
                total = gaps[k] if sign > 0 else -gaps[k]
            else:
                total = total + gaps[k] if sign > 0 else total - gaps[k]
        comps.append(total * inverse)
    return density, comps


def collide(dist):
    density, comps = moments(dist)
    base = 1.0 - 1.5 * (comps[0] * comps[0] + comps[1] * comps[1] + comps[2] * comps[2])
    gain = 1.0 / RELAX_TIME
    keep = 1.0 - gain
    out = [None] * 19
    out[0] = keep * dist[0] + (gain * LATTICE_WEIGHTS[0]) * density * base
    scaled = {w: (gain * w) * density for w in (1.0 / 18.0, 1.0 / 36.0)}
    for k in range(1, 19, 2):
        proj = None
        for axis in range(3):
            sign = LATTICE_DIRS[k][axis]
            if sign == 0:
                continue
            if proj is None:
                proj = comps[axis] if sign > 0 else -comps[axis]
            else:
                proj = proj + comps[axis] if sign > 0 else proj - comps[axis]
        amount = scaled[LATTICE_WEIGHTS[k]]
        even = amount * (base + 4.5 * (proj * proj))
        odd = amount * (3.0 * proj)
        out[k] = keep * dist[k] + (even + odd)
        out[k + 1] = keep * dist[k + 1] + (even - odd)
    return out


def shift_depth(value, amount):
    if amount == 0:
        return value
    return pltpu.roll(value, amount % value.shape[1], 1)


def block_rows(block):
    return pl.multiple_of(block * 8, 8)


def rows_behind(ref, lead, rows, amount):
    here = ref[(*lead, pl.ds(rows + PAD, 8), slice(None))]
    if amount == 0:
        return here
    sub = lax.broadcasted_iota(jnp.int32, here.shape, 0)
    beyond = ref[(*lead, pl.ds(rows + (PAD - 8 * amount), 8), slice(None))]
    mixed = jnp.where(sub == (7 if amount > 0 else 0), beyond, here)
    return pltpu.roll(mixed, amount % 8, 0)


def streamed(post, bits, plane, block):
    rows = block_rows(block)
    flags = bits[plane - 1, pl.ds(rows, 8), :]
    out = []
    for k in range(19):
        dirx, diry, dirz = LATTICE_DIRS[k]
        source = rows_behind(post, (plane - dirx, SLOT[k]), rows, diry)
        if k == 0:
            own = source
        else:
            own = post[plane, SLOT[OPPOSITE_DIR[k]], pl.ds(rows + PAD, 8), :]
        source = shift_depth(source, dirz)
        out.append(jnp.where((flags & (1 << k)) != 0, source, own))
    return out


def store_post(post, plane, block, values):
    for k in range(19):
        post[plane, SLOT[k], pl.ds(block_rows(block) + PAD, 8), :] = values[k]


def pair_patch(g, tiles, beads, noise, force, cols, noise_t):
    bead_tiles = beads.shape[1]
    pairs = noise.shape[1]
    tile = noise.shape[2]
    for t in range(bead_tiles):
        turned = beads[g, t].T
        for c in range(6):
            cols[t, c] = jnp.broadcast_to(turned[:, c : c + 1], (tile, tile))
    sub = lax.broadcasted_iota(jnp.int32, (tile, tile), 0)
    lane = lax.broadcasted_iota(jnp.int32, (tile, tile), 1)
    scaled_eye = jnp.where(sub == lane, NOISE_SCALE, 0.0).astype(BF16)
    step = 32

    def one_pair(p, carry):
        first, second = tiles[g, 0, p], tiles[g, 1, p]
        noise_t[...] = lax.dot_general(
            scaled_eye, noise[g, p], (((1,), (1,)), ((), ())), preferred_element_type=F32
        )
        own = beads[g, first]
        own = [jnp.broadcast_to(own[c : c + 1, :], (step, tile)) for c in range(6)]
        sums = [None] * 3
        for start in range(0, tile, step):
            part = slice(start, start + step)
            gap = [own[c] - cols[second, c, part, :] for c in range(6)]
            dist_sq = gap[0] * gap[0] + gap[1] * gap[1] + gap[2] * gap[2] + SOFTENING
            inverse = lax.rsqrt(dist_sq)
            weight = jnp.maximum(0.0, 1.0 - dist_sq * inverse)
            over = weight * inverse
            along = gap[0] * gap[3] + gap[1] * gap[4] + gap[2] * gap[5]
            scalar = over * (REPULSION + noise_t[part, :] - FRICTION * (over * along))
            for c in range(3):
                piece = (scalar * gap[c]).reshape(step // 8, 8, tile).sum(axis=0)
                sums[c] = piece if sums[c] is None else sums[c] + piece
        out = []
        for t in range(bead_tiles):
            for c in range(3):
                out.append(carry[t * 3 + c] + jnp.where(first == t, sums[c], 0.0))
        return tuple(out)

    zero = jnp.zeros((8, tile), F32)
    total = lax.fori_loop(0, pairs, one_pair, (zero,) * (3 * bead_tiles))
    for t in range(bead_tiles):
        for c in range(3):
            force[g, c : c + 1, t * tile : (t + 1) * tile] = total[t * 3 + c].sum(
                axis=0, keepdims=True
            )


def two_parts(value):
    high = value.astype(BF16)
    return high, (value - high.astype(F32)).astype(BF16)


def one_hot(index, size):
    beads = index.shape[1]
    rows = lax.broadcasted_iota(jnp.int32, (size, beads), 0)
    return jnp.where(rows == index, 1.0, 0.0).astype(BF16)


def repeat(count, body):
    lax.fori_loop(0, count, lambda i, _: (body(i), 0)[1], 0)


def step_kernel(
    n_ax,
    n_xs,
    tiles,
    owner,
    pops,
    mask,
    voxel,
    pos,
    vel,
    noise_hbm,
    pops_out,
    new_pos,
    new_vel,
    field,
    cells,
    post_a,
    post_b,
    flags,
    bits,
    noise,
    row_out,
    row_in,
    corner_out,
    corner_in,
    flag_row_out,
    flag_row_in,
    flag_corner_out,
    flag_corner_in,
    vel_in,
    flow,
    flow_out,
    flow_in,
    force,
    table,
    vel_out,
    tiled,
    cols,
    noise_t,
    load_sem,
    noise_sem,
    save_sem,
    near_send,
    near_recv,
    vel_send,
    vel_recv,
    flow_send,
    flow_recv,
):
    size_x, size_y, size_z = mask.shape
    blocks = size_y // 8
    top, bottom = PAD - 1, PAD + size_y
    first_row, last_row = PAD, PAD + size_y - 1
    own_rows = pl.ds(PAD, size_y)
    _, patches, beads = pos.shape
    me_ax, me_xs = lax.axis_index("ax"), lax.axis_index("xs")

    def at(move_ax, move_xs):
        return (lax.rem(me_ax + (move_ax + n_ax), n_ax), lax.rem(me_xs + (move_xs + n_xs), n_xs))

    loads = [
        pltpu.make_async_copy(pops.at[:, x], cells.at[:, x], load_sem.at[x]) for x in range(size_x)
    ]
    for x in (size_x - 1, 0, 1, 2):
        loads[x].start()
    noise_load = pltpu.make_async_copy(noise_hbm, noise, noise_sem)
    noise_load.start()

    partners = [at(1, 0), at(-1, 0)] + [at(0, d) for d in range(1, n_xs)]
    partners += [at(a, b) for a in (1, -1) for b in (1, -1)]
    barrier = pltpu.get_barrier_semaphore()
    for partner in partners:
        pl.semaphore_signal(barrier, inc=1, device_id=partner, device_id_type=MESH)

    tile = noise.shape[2]
    for g in range(patches):
        for c in range(3):
            vel_out[g, c : c + 1, :] = vel[c, g : g + 1, :]
            for t in range(beads // tile):
                span = slice(t * tile, (t + 1) * tile)
                tiled[g, t, c : c + 1, :] = pos[c, g : g + 1, span]
                tiled[g, t, c + 3 : c + 4, :] = vel[c, g : g + 1, span]

    for x in range(size_x):
        plane = mask[x].astype(F32)
        flags[x + 1, own_rows, :] = plane
        flag_row_out[0, x : x + 1, :] = plane[size_y - 1 : size_y, :]
        flag_row_out[1, x : x + 1, :] = plane[0:1, :]
    for c, k in enumerate(CORNERS):
        dirx, diry, _ = LATTICE_DIRS[k]
        x = size_x if dirx > 0 else 1
        y = last_row if diry > 0 else first_row
        flag_corner_out[c] = flags[x, y : y + 1, :]
    pl.semaphore_wait(barrier, len(partners))

    def exchange(part, faces, row_bufs, corner_bufs):
        targets = [at(1, 0), at(-1, 0), at(0, 1), at(0, -1)]
        targets += [at(LATTICE_DIRS[k][0], LATTICE_DIRS[k][1]) for k in CORNERS]
        ends = list(faces)
        ends += [(row_bufs[0].at[s], row_bufs[1].at[s]) for s in range(2)]
        ends += [(corner_bufs[0].at[c], corner_bufs[1].at[c]) for c in range(4)]
        return [
            pltpu.make_async_remote_copy(
                src_ref=src,
                dst_ref=dst,
                send_sem=near_send.at[part, i],
                recv_sem=near_recv.at[part, i],
                device_id=targets[i],
                device_id_type=MESH,
            )
            for i, (src, dst) in enumerate(ends)
        ]

    flag_copies = exchange(
        0,
        [
            (flags.at[size_x, own_rows], flags.at[0, own_rows]),
            (flags.at[1, own_rows], flags.at[size_x + 1, own_rows]),
        ],
        (flag_row_out, flag_row_in),
        (flag_corner_out, flag_corner_in),
    )
    for copy in flag_copies:
        copy.start()

    def to_group(source, target, send, recv):
        return [
            pltpu.make_async_remote_copy(
                src_ref=source.at[at(0, d)[1]],
                dst_ref=target.at[me_xs],
                send_sem=send.at[d - 1],
                recv_sem=recv.at[d - 1],
                device_id=at(0, d),
                device_id_type=MESH,
            )
            for d in range(1, n_xs)
        ]

    vel_copies = to_group(vel_out, vel_in, vel_send, vel_recv)
    for copy in vel_copies:
        copy.start()
    vel_in[me_xs] = vel_out[me_xs]

    def post_copies(part, post):
        return exchange(
            part,
            [
                (post.at[size_x, 14:19, own_rows], post.at[0, 14:19, own_rows]),
                (post.at[1, 0:5, own_rows], post.at[size_x + 1, 0:5, own_rows]),
            ],
            (row_out.at[part - 1], row_in.at[part - 1]),
            (corner_out.at[part - 1], corner_in.at[part - 1]),
        )

    def pack_rows(part, post):
        for i, k in enumerate(PLUS_Y):
            for x in range(size_x):
                row_out[part - 1, 0, i, x : x + 1, :] = post[
                    x + 1, SLOT[k], last_row : last_row + 1, :
                ]
        for i, k in enumerate(MINUS_Y):
            for x in range(size_x):
                row_out[part - 1, 1, i, x : x + 1, :] = post[
                    x + 1, SLOT[k], first_row : first_row + 1, :
                ]
        for c, k in enumerate(CORNERS):
            dirx, diry, _ = LATTICE_DIRS[k]
            x = size_x if dirx > 0 else 1
            y = last_row if diry > 0 else first_row
            corner_out[part - 1, c] = post[x, SLOT[k], y : y + 1, :]

    def unpack_rows(part, post):
        for i, k in enumerate(PLUS_Y):
            for x in range(size_x):
                post[x + 1, SLOT[k], top : top + 1, :] = row_in[part - 1, 0, i, x : x + 1, :]
        for i, k in enumerate(MINUS_Y):
            for x in range(size_x):
                post[x + 1, SLOT[k], bottom : bottom + 1, :] = row_in[part - 1, 1, i, x : x + 1, :]
        for c, k in enumerate(CORNERS):
            dirx, diry, _ = LATTICE_DIRS[k]
            x = 0 if dirx > 0 else size_x + 1
            y = top if diry > 0 else bottom
            post[x, SLOT[k], y : y + 1, :] = corner_in[part - 1, c]

    def collide_plane(x):
        def one_block(b):
            values = collide([cells[k, x, pl.ds(block_rows(b), 8), :] for k in range(19)])
            store_post(post_a, x + 1, b, values)

        repeat(blocks, one_block)

    copies_a = post_copies(1, post_a)
    loads[size_x - 1].wait()
    collide_plane(size_x - 1)
    copies_a[0].start()
    loads[0].wait()
    collide_plane(0)
    copies_a[1].start()
    for x in range(1, size_x - 1):
        loads[x].wait()
        collide_plane(x)
    pack_rows(1, post_a)
    for copy in copies_a[2:]:
        copy.start()

    for copy in flag_copies:
        copy.wait_recv()
    inside_low = me_xs > 0
    inside_high = me_xs < n_xs - 1
    for x in range(size_x):
        flags[x + 1, top : top + 1, :] = jnp.where(inside_low, flag_row_in[0, x : x + 1, :], 0.0)
        flags[x + 1, bottom : bottom + 1, :] = jnp.where(
            inside_high, flag_row_in[1, x : x + 1, :], 0.0
        )
    for c, k in enumerate(CORNERS):
        dirx, diry, _ = LATTICE_DIRS[k]
        x = 0 if dirx > 0 else size_x + 1
        y = top if diry > 0 else bottom
        flags[x, y : y + 1, :] = jnp.where(
            inside_low if diry > 0 else inside_high, flag_corner_in[c], 0.0
        )

    def bits_block(i):
        x, b = i // blocks, i % blocks
        here = block_rows(b)
        lane = lax.broadcasted_iota(jnp.int32, (8, size_z), 1)
        word = jnp.ones((8, size_z), jnp.int32)
        for k in range(1, 19):
            dirx, diry, dirz = LATTICE_DIRS[k]
            source = shift_depth(rows_behind(flags, (x + (1 - dirx),), here, diry), dirz)
            fluid = source > 0.5
            if dirz > 0:
                fluid = fluid & (lane > 0)
            elif dirz < 0:
                fluid = fluid & (lane < size_z - 1)
            word = word | jnp.where(fluid, 1 << k, 0)
        bits[x, pl.ds(here, 8), :] = word

    repeat(size_x * blocks, bits_block)

    def pair_range(start, stop):
        def one(g):
            pair_patch(start + g, tiles, tiled, noise, force, cols, noise_t)

        repeat(stop - start, one)

    noise_load.wait()
    half = patches // 2
    pair_range(0, half)

    for copy in copies_a:
        copy.wait_recv()
    unpack_rows(1, post_a)
    copies_b = post_copies(2, post_b)

    def advance_plane(plane):
        def one_block(b):
            store_post(post_b, plane, b, collide(streamed(post_a, bits, plane, b)))

        repeat(blocks, one_block)

    advance_plane(size_x)
    copies_b[0].start()
    advance_plane(1)
    copies_b[1].start()
    for plane in range(2, size_x):
        advance_plane(plane)
    pack_rows(2, post_b)
    for copy in copies_b[2:]:
        copy.start()

    pair_range(half, patches)

    for copy in copies_b:
        copy.wait_recv()
    unpack_rows(2, post_b)

    saves = [
        pltpu.make_async_copy(cells.at[:, x], pops_out.at[:, x], save_sem.at[x])
        for x in range(size_x)
    ]

    def finish_plane(plane):
        def one_block(b):
            values = streamed(post_b, bits, plane, b)
            here = block_rows(b)
            for k in range(19):
                cells[k, plane - 1, pl.ds(here, 8), :] = values[k]
            _, comps = moments(values)
            for c in range(3):
                table[c, pl.ds(here + (plane - 1) * size_y, 8), :] = comps[c]

        repeat(blocks, one_block)

    for plane in range(1, size_x + 1):
        finish_plane(plane)
        saves[plane - 1].start()

    lines = size_x * size_y

    def gather_patch(g):
        index = voxel[pl.ds(g, 1), :]
        low, high = lax.rem(index, size_z), lax.div(index, size_z)
        hot = one_hot(low, size_z)
        hit = lax.broadcasted_iota(jnp.int32, (lines, beads), 0) == high
        for c in range(3):
            parts = two_parts(table[c])
            got = jnp.dot(parts[0], hot, preferred_element_type=F32) + jnp.dot(
                parts[1], hot, preferred_element_type=F32
            )
            flow[g, c : c + 1, :] = VELOCITY_SCALE * jnp.where(hit, got, 0.0).sum(
                axis=0, keepdims=True
            )

    repeat(patches, gather_patch)
    for s in range(n_xs):
        row = jnp.int32(0)
        for g in range(patches):
            row = jnp.where(owner[g] == s, g, row)
        flow_out[s] = flow[row]
    flow_copies = to_group(flow_out, flow_in, flow_send, flow_recv)
    for copy in flow_copies:
        copy.start()
    flow_in[me_xs] = flow_out[me_xs]

    for copy in vel_copies:
        copy.wait_recv()
    field[...] = jnp.zeros_like(field)

    def scatter_patch(g):
        index = voxel[pl.ds(g, 1), :]
        low, high = lax.rem(index, size_z), lax.div(index, size_z)
        hot_low = one_hot(low, size_z)
        hot_high = one_hot(high, lines)
        reaction = -TIME_STEP * (DRAG_COEFF * (flow[g] - vel_in[owner[g]]))
        for c in range(3):
            line = jnp.broadcast_to(reaction[c : c + 1, :], (lines, beads))
            total = field[c]
            for part in two_parts(line):
                total = total + lax.dot_general(
                    hot_high * part,
                    hot_low,
                    (((1,), (1,)), ((), ())),
                    preferred_element_type=F32,
                )
            field[c] = total

    repeat(patches, scatter_patch)

    for copy in flow_copies:
        copy.wait_recv()
    for g in range(patches):
        drag = DRAG_COEFF * (flow_in[g] - vel_out[g])
        faster = vel_out[g] + TIME_STEP * (force[g] + drag)
        for c in range(3):
            new_vel[c, g : g + 1, :] = faster[c : c + 1, :]
    for c in range(3):
        new_pos[c] = pos[c] + TIME_STEP * new_vel[c]

    for copy in flag_copies + vel_copies + copies_a + copies_b + flow_copies:
        copy.wait_send()
    for copy in saves:
        copy.wait()


def per_device(
    n_ax, n_xs, populations, fluid_mask, patch_voxel, patch_owner, positions, velocities, pair_tiles, pair_noise
):
    size_x, size_y, size_z = fluid_mask.shape
    patches, _, beads = positions.shape
    tile = pair_noise.shape[2]
    count = beads // tile
    vmem = pl.BlockSpec(memory_space=pltpu.VMEM)
    smem = pl.BlockSpec(memory_space=pltpu.SMEM)
    hbm = pl.BlockSpec(memory_space=pl.ANY)
    high = size_y + 2 * PAD
    post = pltpu.VMEM((size_x + 2, 19, high, size_z), F32)
    beads3 = pltpu.VMEM((patches, 3, beads), F32)
    dma = pltpu.SemaphoreType.DMA

    def body(*refs):
        step_kernel(n_ax, n_xs, *refs)

    dist, new_pos, new_vel, field = pl.pallas_call(
        body,
        out_shape=(
            jax.ShapeDtypeStruct(populations.shape, F32),
            jax.ShapeDtypeStruct((3, patches, beads), F32),
            jax.ShapeDtypeStruct((3, patches, beads), F32),
            jax.ShapeDtypeStruct((3, size_x * size_y, size_z), F32),
        ),
        in_specs=[smem, smem, hbm, vmem, vmem, vmem, vmem, hbm],
        out_specs=(hbm, vmem, vmem, vmem),
        scratch_shapes=[
            pltpu.VMEM(populations.shape, F32),
            post,
            post,
            pltpu.VMEM((size_x + 2, high, size_z), F32),
            pltpu.VMEM((size_x, size_y, size_z), jnp.int32),
            pltpu.VMEM(pair_noise.shape, pair_noise.dtype),
            pltpu.VMEM((2, 2, 5, size_x, size_z), F32),
            pltpu.VMEM((2, 2, 5, size_x, size_z), F32),
            pltpu.VMEM((2, 4, 1, size_z), F32),
            pltpu.VMEM((2, 4, 1, size_z), F32),
            pltpu.VMEM((2, size_x, size_z), F32),
            pltpu.VMEM((2, size_x, size_z), F32),
            pltpu.VMEM((4, 1, size_z), F32),
            pltpu.VMEM((4, 1, size_z), F32),
            beads3,
            beads3,
            beads3,
            beads3,
            beads3,
            pltpu.VMEM((3, size_x * size_y, size_z), F32),
            beads3,
            pltpu.VMEM((patches, count, 8, tile), F32),
            pltpu.VMEM((count, 6, tile, tile), F32),
            pltpu.VMEM((tile, tile), F32),
            dma((size_x,)),
            dma,
            dma((size_x,)),
            dma((3, 8)),
            dma((3, 8)),
            dma((n_xs - 1,)),
            dma((n_xs - 1,)),
            dma((n_xs - 1,)),
            dma((n_xs - 1,)),
        ],
        compiler_params=pltpu.CompilerParams(
            collective_id=0, has_side_effects=True, vmem_limit_bytes=60 * 2**20
        ),
    )(
        jnp.transpose(pair_tiles, (0, 2, 1)),
        patch_owner,
        populations,
        fluid_mask,
        patch_voxel,
        jnp.transpose(positions, (1, 0, 2)),
        jnp.transpose(velocities, (1, 0, 2)),
        pair_noise,
    )
    new_pos, new_vel = (jnp.transpose(x, (1, 0, 2)) for x in (new_pos, new_vel))
    return (dist, new_pos, new_vel, field.reshape(3, size_x, size_y, size_z))


def solution(mesh):
    n_ax, n_xs = mesh.shape["ax"], mesh.shape["xs"]

    def step(*args):
        return per_device(n_ax, n_xs, *args)

    return jax.shard_map(
        step,
        mesh=mesh,
        in_specs=(
            P(None, "ax", "xs", None),
            P("ax", "xs", None),
            P(("ax", "xs"), None),
            P(("ax", "xs")),
            P(("ax", "xs"), None, None),
            P(("ax", "xs"), None, None),
            P(("ax", "xs"), None, None),
            P(("ax", "xs"), None, None, None),
        ),
        out_specs=(
            P(None, "ax", "xs", None),
            P(("ax", "xs"), None, None),
            P(("ax", "xs"), None, None),
            P(None, "ax", "xs", None),
        ),
        check_vma=False,
    )
```

time: 232 us -> 64.5 us (0.28)
  the two profiles are of different devices: /device:TPU:1 before, /device:TPU:7 now
where the time goes in v2:
time: 64.5 us; the launch traced here: 64.4 us
  Pallas kernels  56.2 us (87%)
  local copies, waits for them, and re-layouts  7.51 us (12%)
  between operations  0.67 us (1%)
    pallas_call x1, Pallas kernels, per_device(): pl.pallas_call(body, out_shape=(jax.ShapeDtypeStruct(populations.shape, F...  56.2 us
    unnamed x10, local copies, waits for them, and re-layouts  7.51 us

profile of v2, /device:TPU:7, one launch (start us, length us, event | category | flops | bytes accessed | tf_op | source)
XLA Modules:
  0.0 64.4 jit_solution(14603802097718237564)
XLA Ops:
  0.6 56.2 %shard_map.111 = (f32[19,4,64,256]{3,2,1,0:T(8,128)}, f32[3,8,512]{2,1,0:T(8,128)}, f32[3,8,512]{2,1,0:T(8,128)}, f32[3,256,256]{2,1,0:T(8,128)}) custom-call(s32[8,2,8]{2,1,0:T(2,128)} %bitcast.11, s32[8]{0:T(128)} %refs_1_.1, f32[19,4,64,256]{3,2,1,0:T(8,128)} %refs_2_.1, s32[4,64,256]{2,1,0:T(8,128)} %refs_3_.1, s32[8,512]{1,0:T(8,128)} %refs_4_.1, ...), custom_call_target="tpu_custom_call" | custom-call | tf_op jit(solution)/shard_map/pallas_call | solution.py:586
  56.9 0.0 copy-start.2
  56.9 0.0 copy-start.1
  56.9 0.0 copy-start
  56.9 5.4 %copy.16 = f32[19,4,64,256]{3,2,1,0:T(8,128)} copy(f32[19,4,64,256]{3,2,1,0:T(8,128)} %get-tuple-element.16) | data formatting | bytes 9961472
  62.3 0.0 copy-done.2
  62.3 0.6 copy.17
  62.9 0.0 copy-done.1
  62.9 0.6 copy.18
  63.5 0.0 copy-done
  63.5 0.9 %copy.19 = f32[3,4,64,256]{3,2,1,0:T(8,128)} copy(f32[3,4,64,256]{3,2,1,0:T(8,128)S(1)} %bitcast.6) | data formatting | bytes 1572864
Async XLA Ops:
  56.9 5.4 %copy-start.2 = (f32[3,8,512]{2,1,0:T(8,128)S(1)}, f32[3,8,512]{2,1,0:T(8,128)}, u32[]{:S(2)}) copy-start(f32[3,8,512]{2,1,0:T(8,128)} %get-tuple-element.9) | copy-start | bytes 147460
  56.9 6.0 %copy-start.1 = (f32[3,8,512]{2,1,0:T(8,128)S(1)}, f32[3,8,512]{2,1,0:T(8,128)}, u32[]{:S(2)}) copy-start(f32[3,8,512]{2,1,0:T(8,128)} %get-tuple-element.10) | copy-start | bytes 147460
  56.9 6.6 %copy-start = (f32[3,256,256]{2,1,0:T(8,128)S(1)}, f32[3,256,256]{2,1,0:T(8,128)}, u32[]{:S(2)}) copy-start(f32[3,256,256]{2,1,0:T(8,128)} %get-tuple-element.11) | copy-start | bytes 2359300

commit v3 on v2

v3 whole, which is shorter than its diff:
```python
import jax
import jax.numpy as jnp
from jax import lax
from jax.experimental import pallas as pl
from jax.experimental.pallas import tpu as pltpu
from jax.sharding import PartitionSpec as P

LATTICE_DIRS = [
    (0, 0, 0),
    (1, 0, 0),
    (-1, 0, 0),
    (0, 1, 0),
    (0, -1, 0),
    (0, 0, 1),
    (0, 0, -1),
    (1, 1, 0),
    (-1, -1, 0),
    (1, -1, 0),
    (-1, 1, 0),
    (1, 0, 1),
    (-1, 0, -1),
    (1, 0, -1),
    (-1, 0, 1),
    (0, 1, 1),
    (0, -1, -1),
    (0, 1, -1),
    (0, -1, 1),
]
LATTICE_WEIGHTS = [1.0 / 3.0] + [1.0 / 18.0] * 6 + [1.0 / 36.0] * 12
OPPOSITE_DIR = [0, 2, 1, 4, 3, 6, 5, 8, 7, 10, 9, 12, 11, 14, 13, 16, 15, 18, 17]
ORDER = [k for sign in (-1, 0, 1) for k in range(19) if LATTICE_DIRS[k][0] == sign]
SLOT = [ORDER.index(k) for k in range(19)]
PLUS_Y = [k for k in range(19) if LATTICE_DIRS[k][1] == 1]
MINUS_Y = [k for k in range(19) if LATTICE_DIRS[k][1] == -1]
CORNERS = [7, 8, 9, 10]
RELAX_TIME = 0.8
TIME_STEP = 0.04
REPULSION = 25.0
FRICTION = 4.5
NOISE_AMP = 3.0
NOISE_SCALE = 15.0
DRAG_COEFF = 12.5
VELOCITY_SCALE = 20.0
SOFTENING = 0.01
BF16 = jnp.bfloat16
F32 = jnp.float32
MESH = pl.DeviceIdType.MESH
PAD = 8


def moments(dist):
    density = dist[0]
    gaps = {}
    for k in range(1, 19, 2):
        density = density + (dist[k] + dist[k + 1])
        gaps[k] = dist[k] - dist[k + 1]
    inverse = 1.0 / density
    comps = []
    for axis in range(3):
        total = None
        for k in range(1, 19, 2):
            sign = LATTICE_DIRS[k][axis]
            if sign == 0:
                continue
            if total is None:
                total = gaps[k] if sign > 0 else -gaps[k]
            else:
                total = total + gaps[k] if sign > 0 else total - gaps[k]
        comps.append(total * inverse)
    return density, comps


def collide(dist):
    density, comps = moments(dist)
    base = 1.0 - 1.5 * (comps[0] * comps[0] + comps[1] * comps[1] + comps[2] * comps[2])
    gain = 1.0 / RELAX_TIME
    keep = 1.0 - gain
    out = [None] * 19
    out[0] = keep * dist[0] + (gain * LATTICE_WEIGHTS[0]) * density * base
    scaled = {w: (gain * w) * density for w in (1.0 / 18.0, 1.0 / 36.0)}
    for k in range(1, 19, 2):
        proj = None
        for axis in range(3):
            sign = LATTICE_DIRS[k][axis]
            if sign == 0:
                continue
            if proj is None:
                proj = comps[axis] if sign > 0 else -comps[axis]
            else:
                proj = proj + comps[axis] if sign > 0 else proj - comps[axis]
        amount = scaled[LATTICE_WEIGHTS[k]]
        even = amount * (base + 4.5 * (proj * proj))
        odd = amount * (3.0 * proj)
        out[k] = keep * dist[k] + (even + odd)
        out[k + 1] = keep * dist[k + 1] + (even - odd)
    return out


def shift_depth(value, amount):
    if amount == 0:
        return value
    return pltpu.roll(value, amount % value.shape[1], 1)


def block_rows(block):
    return pl.multiple_of(block * 8, 8)


def rows_behind(ref, lead, rows, amount):
    here = ref[(*lead, pl.ds(rows + PAD, 8), slice(None))]
    if amount == 0:
        return here
    sub = lax.broadcasted_iota(jnp.int32, here.shape, 0)
    beyond = ref[(*lead, pl.ds(rows + (PAD - 8 * amount), 8), slice(None))]
    mixed = jnp.where(sub == (7 if amount > 0 else 0), beyond, here)
    return pltpu.roll(mixed, amount % 8, 0)


def streamed(post, bits, plane, block):
    rows = block_rows(block)
    flags = bits[plane - 1, pl.ds(rows, 8), :]
    out = []
    for k in range(19):
        dirx, diry, dirz = LATTICE_DIRS[k]
        source = rows_behind(post, (plane - dirx, SLOT[k]), rows, diry)
        if k == 0:
            own = source
        else:
            own = post[plane, SLOT[OPPOSITE_DIR[k]], pl.ds(rows + PAD, 8), :]
        source = shift_depth(source, dirz)
        out.append(jnp.where((flags & (1 << k)) != 0, source, own))
    return out


def store_post(post, plane, block, values):
    for k in range(19):
        post[plane, SLOT[k], pl.ds(block_rows(block) + PAD, 8), :] = values[k]


def pair_patch(g, tiles, beads, noise, force, cols, noise_t):
    bead_tiles = beads.shape[1]
    pairs = noise.shape[1]
    tile = noise.shape[2]
    sub = lax.broadcasted_iota(jnp.int32, (tile, tile), 0)
    lane = lax.broadcasted_iota(jnp.int32, (tile, tile), 1)
    scaled_eye = jnp.where(sub == lane, NOISE_SCALE, 0.0).astype(BF16)
    for p in range(pairs):
        noise_t[p] = lax.dot_general(
            scaled_eye, noise[g, p], (((1,), (1,)), ((), ())), preferred_element_type=F32
        )
    for t in range(bead_tiles):
        turned = beads[g, t].T
        for c in range(6):
            cols[t, c] = jnp.broadcast_to(turned[:, c : c + 1], (tile, tile))
    step = 32

    def one_pair(p, carry):
        first, second = tiles[g, 0, p], tiles[g, 1, p]
        own = beads[g, first]
        own = [jnp.broadcast_to(own[c : c + 1, :], (step, tile)) for c in range(6)]
        sums = [None] * 3
        for start in range(0, tile, step):
            part = slice(start, start + step)
            gap = [own[c] - cols[second, c, part, :] for c in range(6)]
            dist_sq = (gap[0] * gap[0] + gap[1] * gap[1]) + (gap[2] * gap[2] + SOFTENING)
            over = jnp.maximum(0.0, lax.rsqrt(dist_sq) - 1.0)
            along = gap[0] * gap[3] + gap[1] * gap[4] + gap[2] * gap[5]
            scalar = over * ((REPULSION + noise_t[p, part, :]) - over * along)
            for c in range(3):
                piece = (scalar * gap[c]).reshape(step // 8, 8, tile).sum(axis=0)
                sums[c] = piece if sums[c] is None else sums[c] + piece
        out = []
        for t in range(bead_tiles):
            for c in range(3):
                out.append(carry[t * 3 + c] + jnp.where(first == t, sums[c], 0.0))
        return tuple(out)

    def two_pairs(p, carry):
        return one_pair(2 * p + 1, one_pair(2 * p, carry))

    zero = jnp.zeros((8, tile), F32)
    total = lax.fori_loop(0, pairs // 2, two_pairs, (zero,) * (3 * bead_tiles))
    for t in range(bead_tiles):
        for c in range(3):
            force[g, c : c + 1, t * tile : (t + 1) * tile] = total[t * 3 + c].sum(
                axis=0, keepdims=True
            )


def two_parts(value):
    high = value.astype(BF16)
    return high, (value - high.astype(F32)).astype(BF16)


def one_hot(index, size):
    beads = index.shape[1]
    rows = lax.broadcasted_iota(jnp.int32, (size, beads), 0)
    return jnp.where(rows == index, 1.0, 0.0).astype(BF16)


def repeat(count, body):
    lax.fori_loop(0, count, lambda i, _: (body(i), 0)[1], 0)


def step_kernel(
    n_ax,
    n_xs,
    tiles_hbm,
    owner_hbm,
    pops,
    mask_hbm,
    voxel_hbm,
    pos_hbm,
    vel_hbm,
    noise_hbm,
    pops_out,
    new_pos,
    new_vel,
    field,
    tiles,
    owner,
    mask,
    voxel,
    pos,
    vel,
    hot_low,
    hot_high,
    parts,
    cells,
    post_a,
    post_b,
    flags,
    bits,
    noise,
    row_out_a,
    row_in_a,
    corner_out_a,
    corner_in_a,
    row_out_b,
    row_in_b,
    corner_out_b,
    corner_in_b,
    scaled,
    vel_in,
    flow,
    flow_out,
    flow_in,
    force,
    table,
    vel_out,
    tiled,
    cols,
    noise_t,
    load_sem,
    small_sem,
    save_sem,
    near_send,
    near_recv,
    vel_send,
    vel_recv,
    flow_send,
    flow_recv,
):
    size_x, size_y, size_z = mask_hbm.shape
    blocks = size_y // 8
    top, bottom = PAD - 1, PAD + size_y
    first_row, last_row = PAD, PAD + size_y - 1
    own_rows = pl.ds(PAD, size_y)
    _, patches, beads = pos_hbm.shape
    me_ax, me_xs = lax.axis_index("ax"), lax.axis_index("xs")

    def at(move_ax, move_xs):
        return (lax.rem(me_ax + (move_ax + n_ax), n_ax), lax.rem(me_xs + (move_xs + n_xs), n_xs))

    loads = [
        pltpu.make_async_copy(pops.at[:, x], cells.at[:, x], load_sem.at[x]) for x in range(size_x)
    ]
    smalls = [
        pltpu.make_async_copy(src, dst, small_sem.at[i])
        for i, (src, dst) in enumerate(
            [
                (mask_hbm, mask),
                (pos_hbm, pos),
                (vel_hbm, vel),
                (voxel_hbm, voxel),
                (tiles_hbm, tiles),
                (owner_hbm, owner),
                (noise_hbm, noise),
            ]
        )
    ]
    loads[size_x - 1].start()
    loads[0].start()
    for copy in smalls[:-1]:
        copy.start()
    for x in range(1, size_x - 1):
        loads[x].start()
    smalls[-1].start()

    partners = [at(1, 0), at(-1, 0)] + [at(0, d) for d in range(1, n_xs)]
    partners += [at(a, b) for a in (1, -1) for b in (1, -1)]
    barrier = pltpu.get_barrier_semaphore()
    for partner in partners:
        pl.semaphore_signal(barrier, inc=1, device_id=partner, device_id_type=MESH)

    def remote(src, dst, sems, spot, target):
        return pltpu.make_async_remote_copy(
            src_ref=src,
            dst_ref=dst,
            send_sem=sems[0].at[spot],
            recv_sem=sems[1].at[spot],
            device_id=target,
            device_id_type=MESH,
        )

    near = (near_send, near_recv)
    flag_copies = [
        remote(flags.at[size_x, own_rows], flags.at[0, own_rows], near, (0, 0), at(1, 0)),
        remote(flags.at[1, own_rows], flags.at[size_x + 1, own_rows], near, (0, 1), at(-1, 0)),
    ]

    def to_group(source, target, send, recv):
        return [
            pltpu.make_async_remote_copy(
                src_ref=source.at[at(0, d)[1]],
                dst_ref=target.at[me_xs],
                send_sem=send.at[d - 1],
                recv_sem=recv.at[d - 1],
                device_id=at(0, d),
                device_id_type=MESH,
            )
            for d in range(1, n_xs)
        ]

    def post_copies(part, post, row_bufs, corner_bufs):
        ends = [
            (post.at[size_x, 14:19, own_rows], post.at[0, 14:19, own_rows], at(1, 0)),
            (post.at[1, 0:5, own_rows], post.at[size_x + 1, 0:5, own_rows], at(-1, 0)),
        ]
        for side in range(2):
            ends.append((row_bufs[0].at[side], row_bufs[1].at[side], at(0, 1 - 2 * side)))
        for c, k in enumerate(CORNERS):
            target = at(LATTICE_DIRS[k][0], LATTICE_DIRS[k][1])
            ends.append((corner_bufs[0].at[c], corner_bufs[1].at[c], target))
        return [
            remote(src, dst, near, (part, i), target) for i, (src, dst, target) in enumerate(ends)
        ]

    def corner_spots(c, halo):
        dirx, diry, _ = LATTICE_DIRS[CORNERS[c]]
        if halo:
            return (0 if dirx > 0 else size_x + 1), (top if diry > 0 else bottom)
        return (size_x if dirx > 0 else 1), (last_row if diry > 0 else first_row)

    def pack_rows(post, row_buf, corner_buf):
        for side, dirs in enumerate((PLUS_Y, MINUS_Y)):
            y = first_row if side else last_row
            for i, k in enumerate(dirs):
                for x in range(size_x):
                    row_buf[side, i, x : x + 1, :] = post[x + 1, SLOT[k], y : y + 1, :]
        for c, k in enumerate(CORNERS):
            x, y = corner_spots(c, False)
            corner_buf[c, 0:1, :] = post[x, SLOT[k], y : y + 1, :]

    def unpack_rows(post, row_buf, corner_buf):
        for side, dirs in enumerate((PLUS_Y, MINUS_Y)):
            y = bottom if side else top
            for i, k in enumerate(dirs):
                for x in range(size_x):
                    post[x + 1, SLOT[k], y : y + 1, :] = row_buf[side, i, x : x + 1, :]
        for c, k in enumerate(CORNERS):
            x, y = corner_spots(c, True)
            post[x, SLOT[k], y : y + 1, :] = corner_buf[c, 0:1, :]

    def collide_plane(x):
        def one_block(b):
            values = collide([cells[k, x, pl.ds(block_rows(b), 8), :] for k in range(19)])
            store_post(post_a, x + 1, b, values)

        repeat(blocks, one_block)

    rows_a, corners_a = (row_out_a, row_in_a), (corner_out_a, corner_in_a)
    rows_b, corners_b = (row_out_b, row_in_b), (corner_out_b, corner_in_b)
    copies_a = post_copies(1, post_a, rows_a, corners_a)
    copies_b = post_copies(2, post_b, rows_b, corners_b)

    smalls[0].wait()
    for x in range(size_x):
        plane = mask[x].astype(F32)
        flags[x + 1, own_rows, :] = plane
        row_out_a[0, 5, x : x + 1, :] = plane[size_y - 1 : size_y, :]
        row_out_a[1, 5, x : x + 1, :] = plane[0:1, :]
    for c in range(4):
        x, y = corner_spots(c, False)
        corner_out_a[c, 1:2, :] = flags[x, y : y + 1, :]

    loads[size_x - 1].wait()
    collide_plane(size_x - 1)
    pl.semaphore_wait(barrier, len(partners))
    copies_a[0].start()
    loads[0].wait()
    collide_plane(0)
    copies_a[1].start()
    for copy in flag_copies:
        copy.start()
    for x in range(1, size_x - 1):
        loads[x].wait()
        collide_plane(x)
    pack_rows(post_a, row_out_a, corner_out_a)
    for copy in copies_a[2:]:
        copy.start()

    tile = noise.shape[2]
    smalls[1].wait()
    smalls[2].wait()
    for g in range(patches):
        for c in range(3):
            vel_out[g, c : c + 1, :] = vel[c, g : g + 1, :]
            for t in range(beads // tile):
                span = slice(t * tile, (t + 1) * tile)
                tiled[g, t, c : c + 1, :] = pos[c, g : g + 1, span]
                tiled[g, t, c + 3 : c + 4, :] = FRICTION * vel[c, g : g + 1, span]

    vel_copies = to_group(vel_out, vel_in, vel_send, vel_recv)
    for copy in vel_copies:
        copy.start()
    vel_in[me_xs] = vel_out[me_xs]

    def bits_block(i):
        x, b = i // blocks, i % blocks
        here = block_rows(b)
        lane = lax.broadcasted_iota(jnp.int32, (8, size_z), 1)
        word = jnp.ones((8, size_z), jnp.int32)
        for k in range(1, 19):
            dirx, diry, dirz = LATTICE_DIRS[k]
            source = shift_depth(rows_behind(flags, (x + (1 - dirx),), here, diry), dirz)
            fluid = source > 0.5
            if dirz > 0:
                fluid = fluid & (lane > 0)
            elif dirz < 0:
                fluid = fluid & (lane < size_z - 1)
            word = word | jnp.where(fluid, 1 << k, 0)
        bits[x, pl.ds(here, 8), :] = word

    def pair_range(start, stop):
        def one(g):
            pair_patch(start + g, tiles, tiled, noise, force, cols, noise_t)

        repeat(stop - start, one)

    lines = size_x * size_y
    smalls[3].wait()

    def hot_patch(g):
        index = voxel[pl.ds(g, 1), :]
        hot_low[g] = one_hot(lax.rem(index, size_z), size_z)
        hot_high[g] = one_hot(lax.div(index, size_z), lines)

    repeat(patches, hot_patch)

    for copy in smalls[4:]:
        copy.wait()
    early = patches // 2 - 1
    pair_range(0, early)

    for copy in flag_copies:
        copy.wait_recv()
    for copy in copies_a[2:]:
        copy.wait_recv()
    unpack_rows(post_a, row_in_a, corner_in_a)
    inside = (me_xs > 0, me_xs < n_xs - 1)
    for side in range(2):
        y = bottom if side else top
        for x in range(size_x):
            flags[x + 1, y : y + 1, :] = jnp.where(
                inside[side], row_in_a[side, 5, x : x + 1, :], 0.0
            )
    for c, k in enumerate(CORNERS):
        x, y = corner_spots(c, True)
        flags[x, y : y + 1, :] = jnp.where(
            inside[0 if LATTICE_DIRS[k][1] > 0 else 1], corner_in_a[c, 1:2, :], 0.0
        )
    repeat(size_x * blocks, bits_block)

    def advance_plane(plane):
        def one_block(b):
            store_post(post_b, plane, b, collide(streamed(post_a, bits, plane, b)))

        repeat(blocks, one_block)

    for plane in range(2, size_x):
        advance_plane(plane)
    copies_a[0].wait_recv()
    copies_a[1].wait_recv()
    advance_plane(size_x)
    copies_b[0].start()
    advance_plane(1)
    copies_b[1].start()
    pack_rows(post_b, row_out_b, corner_out_b)
    for copy in copies_b[2:]:
        copy.start()

    pair_range(early, patches)

    saves = [
        pltpu.make_async_copy(cells.at[:, x], pops_out.at[:, x], save_sem.at[x])
        for x in range(size_x)
    ]

    def finish_plane(plane):
        def one_block(b):
            values = streamed(post_b, bits, plane, b)
            here = block_rows(b)
            for k in range(19):
                cells[k, plane - 1, pl.ds(here, 8), :] = values[k]
            _, comps = moments(values)
            for c in range(3):
                table[plane - 1, c, pl.ds(here, 8), :] = comps[c]

        repeat(blocks, one_block)
        saves[plane - 1].start()

    def gather_planes(planes, first):
        low_line, high_line = planes[0] * size_y, planes[1] * size_y
        for n, plane in enumerate(planes):
            for c in range(3):
                spot = pl.ds((2 * c + n) * size_y, size_y)
                parts[0, spot, :], parts[1, spot, :] = two_parts(table[plane, c])

        def gather_patch(g):
            line = lax.div(voxel[pl.ds(g, 1), :], size_z)
            line = jnp.where(
                line >= high_line,
                jnp.where(line < high_line + size_y, line - (high_line - size_y), -1),
                jnp.where(line < low_line + size_y, line - low_line, -1),
            )
            hit = lax.broadcasted_iota(jnp.int32, (2 * size_y, beads), 0) == line
            got = jnp.dot(parts[0], hot_low[g], preferred_element_type=F32)
            got = got + jnp.dot(parts[1], hot_low[g], preferred_element_type=F32)
            for c in range(3):
                piece = got[2 * c * size_y : 2 * (c + 1) * size_y]
                piece = VELOCITY_SCALE * jnp.where(hit, piece, 0.0).sum(axis=0, keepdims=True)
                if first:
                    flow[g, c : c + 1, :] = piece
                else:
                    flow[g, c : c + 1, :] = flow[g, c : c + 1, :] + piece

        repeat(patches, gather_patch)

    for copy in copies_b[2:]:
        copy.wait_recv()
    unpack_rows(post_b, row_in_b, corner_in_b)
    finish_plane(2)
    finish_plane(3)
    gather_planes((1, 2), True)
    copies_b[0].wait_recv()
    copies_b[1].wait_recv()
    finish_plane(1)
    finish_plane(size_x)
    gather_planes((0, size_x - 1), False)
    for s in range(n_xs):
        row = jnp.int32(0)
        for g in range(patches):
            row = jnp.where(owner[g] == s, g, row)
        flow_out[s] = flow[row]
    flow_copies = to_group(flow_out, flow_in, flow_send, flow_recv)
    for copy in flow_copies:
        copy.start()
    flow_in[me_xs] = flow_out[me_xs]

    for copy in vel_copies:
        copy.wait_recv()
    def scatter_patch(g):
        reaction = -TIME_STEP * (DRAG_COEFF * (flow[g] - vel_in[owner[g]]))
        hot = hot_high[g].reshape(lines // 16, 16, beads)
        for c in range(3):
            line = jnp.broadcast_to(reaction[c : c + 1, :], (16, beads))
            for n, part in enumerate(two_parts(line)):
                scaled[n, c * lines : (c + 1) * lines, :] = (hot * part[None]).reshape(lines, beads)
        both = (((1,), (1,)), ((), ()))
        total = lax.dot_general(scaled[0], hot_low[g], both, preferred_element_type=F32)
        total = total + lax.dot_general(scaled[1], hot_low[g], both, preferred_element_type=F32)
        for c in range(3):
            field[c] = field[c] + total[c * lines : (c + 1) * lines]

    field[...] = jnp.zeros_like(field)
    repeat(patches, scatter_patch)

    for copy in flow_copies:
        copy.wait_recv()
    for g in range(patches):
        drag = DRAG_COEFF * (flow_in[g] - vel_out[g])
        faster = vel_out[g] + TIME_STEP * (force[g] + drag)
        for c in range(3):
            new_vel[c, g : g + 1, :] = faster[c : c + 1, :]
    for c in range(3):
        new_pos[c] = pos[c] + TIME_STEP * new_vel[c]

    for copy in flag_copies + vel_copies + copies_a + copies_b + flow_copies:
        copy.wait_send()
    for copy in saves:
        copy.wait()


def per_device(
    n_ax, n_xs, populations, fluid_mask, patch_voxel, patch_owner, positions, velocities, pair_tiles, pair_noise
):
    size_x, size_y, size_z = fluid_mask.shape
    patches, _, beads = positions.shape
    tile = pair_noise.shape[2]
    count = beads // tile
    vmem = pl.BlockSpec(memory_space=pltpu.VMEM)
    high = size_y + 2 * PAD
    post = pltpu.VMEM((size_x + 2, 19, high, size_z), F32)
    beads3 = pltpu.VMEM((patches, 3, beads), F32)
    dma = pltpu.SemaphoreType.DMA

    def body(*refs):
        step_kernel(n_ax, n_xs, *refs)

    dist, new_pos, new_vel, field = pl.pallas_call(
        body,
        out_shape=(
            jax.ShapeDtypeStruct(populations.shape, F32),
            jax.ShapeDtypeStruct((3, patches, beads), F32),
            jax.ShapeDtypeStruct((3, patches, beads), F32),
            jax.ShapeDtypeStruct((3, size_x * size_y, size_z), F32),
        ),
        in_specs=[pl.BlockSpec(memory_space=pltpu.HBM)] * 8,
        out_specs=(pl.BlockSpec(memory_space=pl.ANY), vmem, vmem, vmem),
        scratch_shapes=[
            pltpu.SMEM((patches, 2, pair_noise.shape[1]), jnp.int32),
            pltpu.SMEM((patches,), jnp.int32),
            pltpu.VMEM((size_x, size_y, size_z), jnp.int32),
            pltpu.VMEM((patches, beads), jnp.int32),
            pltpu.VMEM((3, patches, beads), F32),
            pltpu.VMEM((3, patches, beads), F32),
            pltpu.VMEM((patches, size_z, beads), BF16),
            pltpu.VMEM((patches, size_x * size_y, beads), BF16),
            pltpu.VMEM((2, 6 * size_y, size_z), BF16),
            pltpu.VMEM(populations.shape, F32),
            post,
            post,
            pltpu.VMEM((size_x + 2, high, size_z), F32),
            pltpu.VMEM((size_x, size_y, size_z), jnp.int32),
            pltpu.VMEM(pair_noise.shape, pair_noise.dtype),
            pltpu.VMEM((2, 6, size_x, size_z), F32),
            pltpu.VMEM((2, 6, size_x, size_z), F32),
            pltpu.VMEM((4, 2, size_z), F32),
            pltpu.VMEM((4, 2, size_z), F32),
            pltpu.VMEM((2, 5, size_x, size_z), F32),
            pltpu.VMEM((2, 5, size_x, size_z), F32),
            pltpu.VMEM((4, 1, size_z), F32),
            pltpu.VMEM((4, 1, size_z), F32),
            pltpu.VMEM((2, 3 * size_x * size_y, beads), BF16),
            beads3,
            beads3,
            beads3,
            beads3,
            beads3,
            pltpu.VMEM((size_x, 3, size_y, size_z), F32),
            beads3,
            pltpu.VMEM((patches, count, 8, tile), F32),
            pltpu.VMEM((count, 6, tile, tile), F32),
            pltpu.VMEM((pair_noise.shape[1], tile, tile), F32),
            dma((size_x,)),
            dma((7,)),
            dma((size_x,)),
            dma((3, 8)),
            dma((3, 8)),
            dma((n_xs - 1,)),
            dma((n_xs - 1,)),
            dma((n_xs - 1,)),
            dma((n_xs - 1,)),
        ],
        compiler_params=pltpu.CompilerParams(
            collective_id=0, has_side_effects=True, vmem_limit_bytes=44 * 2**20
        ),
    )(
        *(
            pltpu.with_memory_space_constraint(x, pltpu.HBM)
            for x in (
                jnp.transpose(pair_tiles, (0, 2, 1)),
                patch_owner,
                populations,
                fluid_mask,
                patch_voxel,
                jnp.transpose(positions, (1, 0, 2)),
                jnp.transpose(velocities, (1, 0, 2)),
                pair_noise,
            )
        )
    )
    new_pos, new_vel = (jnp.transpose(x, (1, 0, 2)) for x in (new_pos, new_vel))
    return (dist, new_pos, new_vel, field.reshape(3, size_x, size_y, size_z))


def solution(mesh):
    n_ax, n_xs = mesh.shape["ax"], mesh.shape["xs"]

    def step(*args):
        return per_device(n_ax, n_xs, *args)

    return jax.shard_map(
        step,
        mesh=mesh,
        in_specs=(
            P(None, "ax", "xs", None),
            P("ax", "xs", None),
            P(("ax", "xs"), None),
            P(("ax", "xs")),
            P(("ax", "xs"), None, None),
            P(("ax", "xs"), None, None),
            P(("ax", "xs"), None, None),
            P(("ax", "xs"), None, None, None),
        ),
        out_specs=(
            P(None, "ax", "xs", None),
            P(("ax", "xs"), None, None),
            P(("ax", "xs"), None, None),
            P(None, "ax", "xs", None),
        ),
        check_vma=False,
    )
```

time: 64.5 us -> 56 us (0.87)
  the two profiles are of different devices: /device:TPU:7 before, /device:TPU:1 now
where the time goes in v3:
time: 56 us; the launch traced here: 55.9 us
  Pallas kernels  50.8 us (91%)
  local copies, waits for them, and re-layouts  4.39 us (8%)
  between operations  0.64 us (1%)
    pallas_call x1, Pallas kernels, per_device(): pl.pallas_call(body, out_shape=(jax.ShapeDtypeStruct(populations.shape, F...  50.8 us
    unnamed x4, local copies, waits for them, and re-layouts  4.39 us

profile of v3, /device:TPU:1, one launch (start us, length us, event | category | flops | bytes accessed | tf_op | source)
XLA Modules:
  0.0 55.9 jit_solution(7587109382885614984)
XLA Ops:
  0.6 50.8 %shard_map.111 = (f32[19,4,64,256]{3,2,1,0:T(8,128)S(1)}, f32[3,8,512]{2,1,0:T(8,128)S(1)}, f32[3,8,512]{2,1,0:T(8,128)S(1)}, f32[3,256,256]{2,1,0:T(8,128)S(1)}) custom-call(s32[8,2,8]{2,1,0:T(2,128)} %bitcast.11, s32[8]{0:T(128)} %refs_1_.1, f32[19,4,64,256]{3,2,1,0:T(8,128)} %refs_2_.1, s32[4,64,256]{2,1,0:T(8,128)} %refs_3_.1, s32[8,512]{1,0:T(8,128)} %refs_4_.1, ...), custom_call_target="tpu_custom_call" | custom-call | tf_op jit(solution)/shard_map/pallas_call | solution.py:621
  51.5 2.3 %copy.16 = f32[19,4,64,256]{3,2,1,0:T(8,128)} copy(f32[19,4,64,256]{3,2,1,0:T(8,128)S(1)} %get-tuple-element.16) | data formatting | bytes 9961472
  53.8 0.6 %copy.17 = f32[8,3,512]{2,0,1:T(8,128)} copy(f32[8,3,512]{2,0,1:T(8,128)S(1)} %bitcast.8) | data formatting | bytes 98304
  54.4 0.6 %copy.18 = f32[8,3,512]{2,0,1:T(8,128)} copy(f32[8,3,512]{2,0,1:T(8,128)S(1)} %bitcast.7) | data formatting | bytes 98304
  55.0 0.9 %copy.19 = f32[3,4,64,256]{3,2,1,0:T(8,128)} copy(f32[3,4,64,256]{3,2,1,0:T(8,128)S(1)} %bitcast.6) | data formatting | bytes 1572864

commit v4 on v3

--- a/solution.py
+++ b/solution.py
@@ -198,8 +198,13 @@
     return jnp.where(rows == index, 1.0, 0.0).astype(BF16)
 
 
-def repeat(count, body):
-    lax.fori_loop(0, count, lambda i, _: (body(i), 0)[1], 0)
+def repeat(count, body, together=1):
+    def turn(i, carry):
+        for n in range(together):
+            body(i * together + n)
+        return carry
+
+    lax.fori_loop(0, count // together, turn, 0)
 
 
 def step_kernel(
@@ -377,7 +382,7 @@
             values = collide([cells[k, x, pl.ds(block_rows(b), 8), :] for k in range(19)])
             store_post(post_a, x + 1, b, values)
 
-        repeat(blocks, one_block)
+        repeat(blocks, one_block, 8)
 
     rows_a, corners_a = (row_out_a, row_in_a), (corner_out_a, corner_in_a)
     rows_b, corners_b = (row_out_b, row_in_b), (corner_out_b, corner_in_b)
@@ -456,7 +461,7 @@
         hot_low[g] = one_hot(lax.rem(index, size_z), size_z)
         hot_high[g] = one_hot(lax.div(index, size_z), lines)
 
-    repeat(patches, hot_patch)
+    repeat(patches, hot_patch, 4)
 
     for copy in smalls[4:]:
         copy.wait()
@@ -480,13 +485,13 @@
         flags[x, y : y + 1, :] = jnp.where(
             inside[0 if LATTICE_DIRS[k][1] > 0 else 1], corner_in_a[c, 1:2, :], 0.0
         )
-    repeat(size_x * blocks, bits_block)
+    repeat(size_x * blocks, bits_block, 8)
 
     def advance_plane(plane):
         def one_block(b):
             store_post(post_b, plane, b, collide(streamed(post_a, bits, plane, b)))
 
-        repeat(blocks, one_block)
+        repeat(blocks, one_block, 8)
 
     for plane in range(2, size_x):
         advance_plane(plane)
@@ -517,7 +522,7 @@
             for c in range(3):
                 table[plane - 1, c, pl.ds(here, 8), :] = comps[c]
 
-        repeat(blocks, one_block)
+        repeat(blocks, one_block, 8)
         saves[plane - 1].start()
 
     def gather_planes(planes, first):
@@ -545,7 +550,7 @@
                 else:
                     flow[g, c : c + 1, :] = flow[g, c : c + 1, :] + piece
 
-        repeat(patches, gather_patch)
+        repeat(patches, gather_patch, 4)
 
     for copy in copies_b[2:]:
         copy.wait_recv()
@@ -584,7 +589,7 @@
             field[c] = field[c] + total[c * lines : (c + 1) * lines]
 
     field[...] = jnp.zeros_like(field)
-    repeat(patches, scatter_patch)
+    repeat(patches, scatter_patch, 4)
 
     for copy in flow_copies:
         copy.wait_recv()

time: 56 us -> 46.8 us (0.84)
  Pallas kernels: 50.8 us -> 41.6 us
    pallas_call x1, Pallas kernels: 50.8 us -> 41.6 us  [per_device(): pl.pallas_call(body, out_shape=(jax.ShapeDtypeStruct(populations.shape, F...]
where the time goes in v4:
time: 46.8 us; the launch traced here: 46.7 us
  Pallas kernels  41.6 us (89%)
  local copies, waits for them, and re-layouts  4.39 us (9%)
  between operations  0.64 us (1%)
    pallas_call x1, Pallas kernels, per_device(): pl.pallas_call(body, out_shape=(jax.ShapeDtypeStruct(populations.shape, F...  41.6 us
    unnamed x4, local copies, waits for them, and re-layouts  4.39 us

profile of v4, /device:TPU:1, one launch (start us, length us, event | category | flops | bytes accessed | tf_op | source)
XLA Modules:
  0.0 46.7 jit_solution(1447682911675129247)
XLA Ops:
  0.6 41.6 %shard_map.111 = (f32[19,4,64,256]{3,2,1,0:T(8,128)S(1)}, f32[3,8,512]{2,1,0:T(8,128)S(1)}, f32[3,8,512]{2,1,0:T(8,128)S(1)}, f32[3,256,256]{2,1,0:T(8,128)S(1)}) custom-call(s32[8,2,8]{2,1,0:T(2,128)} %bitcast.11, s32[8]{0:T(128)} %refs_1_.1, f32[19,4,64,256]{3,2,1,0:T(8,128)} %refs_2_.1, s32[4,64,256]{2,1,0:T(8,128)} %refs_3_.1, s32[8,512]{1,0:T(8,128)} %refs_4_.1, ...), custom_call_target="tpu_custom_call" | custom-call | tf_op jit(solution)/shard_map/pallas_call | solution.py:626
  42.3 2.3 %copy.16 = f32[19,4,64,256]{3,2,1,0:T(8,128)} copy(f32[19,4,64,256]{3,2,1,0:T(8,128)S(1)} %get-tuple-element.16) | data formatting | bytes 9961472
  44.5 0.6 %copy.17 = f32[8,3,512]{2,0,1:T(8,128)} copy(f32[8,3,512]{2,0,1:T(8,128)S(1)} %bitcast.8) | data formatting | bytes 98304
  45.2 0.6 %copy.18 = f32[8,3,512]{2,0,1:T(8,128)} copy(f32[8,3,512]{2,0,1:T(8,128)S(1)} %bitcast.7) | data formatting | bytes 98304
  45.8 0.9 %copy.19 = f32[3,4,64,256]{3,2,1,0:T(8,128)} copy(f32[3,4,64,256]{3,2,1,0:T(8,128)S(1)} %bitcast.6) | data formatting | bytes 1572864

commit v5 on v4

--- a/solution.py
+++ b/solution.py
@@ -465,7 +465,7 @@
 
     for copy in smalls[4:]:
         copy.wait()
-    early = patches // 2 - 1
+    early = patches // 2 + 1
     pair_range(0, early)
 
     for copy in flag_copies:

time: 46.8 us -> 45 us (0.962)
  Pallas kernels: 41.6 us -> 39.7 us
    pallas_call x1, Pallas kernels: 41.6 us -> 39.7 us  [per_device(): pl.pallas_call(body, out_shape=(jax.ShapeDtypeStruct(populations.shape, F...]
where the time goes in v5:
time: 45 us; the launch traced here: 44.8 us
  Pallas kernels  39.7 us (88%)
  local copies, waits for them, and re-layouts  4.39 us (10%)
  between operations  0.64 us (1%)
    pallas_call x1, Pallas kernels, per_device(): pl.pallas_call(body, out_shape=(jax.ShapeDtypeStruct(populations.shape, F...  39.7 us
    unnamed x4, local copies, waits for them, and re-layouts  4.39 us

profile of v5, /device:TPU:1, one launch (start us, length us, event | category | flops | bytes accessed | tf_op | source)
XLA Modules:
  0.0 44.8 jit_solution(2419065626656196324)
XLA Ops:
  0.6 39.7 %shard_map.111 = (f32[19,4,64,256]{3,2,1,0:T(8,128)S(1)}, f32[3,8,512]{2,1,0:T(8,128)S(1)}, f32[3,8,512]{2,1,0:T(8,128)S(1)}, f32[3,256,256]{2,1,0:T(8,128)S(1)}) custom-call(s32[8,2,8]{2,1,0:T(2,128)} %bitcast.11, s32[8]{0:T(128)} %refs_1_.1, f32[19,4,64,256]{3,2,1,0:T(8,128)} %refs_2_.1, s32[4,64,256]{2,1,0:T(8,128)} %refs_3_.1, s32[8,512]{1,0:T(8,128)} %refs_4_.1, ...), custom_call_target="tpu_custom_call" | custom-call | tf_op jit(solution)/shard_map/pallas_call | solution.py:626
  40.4 2.3 %copy.16 = f32[19,4,64,256]{3,2,1,0:T(8,128)} copy(f32[19,4,64,256]{3,2,1,0:T(8,128)S(1)} %get-tuple-element.16) | data formatting | bytes 9961472
  42.7 0.6 %copy.17 = f32[8,3,512]{2,0,1:T(8,128)} copy(f32[8,3,512]{2,0,1:T(8,128)S(1)} %bitcast.8) | data formatting | bytes 98304
  43.3 0.6 %copy.18 = f32[8,3,512]{2,0,1:T(8,128)} copy(f32[8,3,512]{2,0,1:T(8,128)S(1)} %bitcast.7) | data formatting | bytes 98304
  43.9 0.9 %copy.19 = f32[3,4,64,256]{3,2,1,0:T(8,128)} copy(f32[3,4,64,256]{3,2,1,0:T(8,128)S(1)} %bitcast.6) | data formatting | bytes 1572864

commit v6 on v5

--- a/solution.py
+++ b/solution.py
@@ -550,7 +550,7 @@
                 else:
                     flow[g, c : c + 1, :] = flow[g, c : c + 1, :] + piece
 
-        repeat(patches, gather_patch, 4)
+        repeat(patches, gather_patch, 8)
 
     for copy in copies_b[2:]:
         copy.wait_recv()
@@ -589,7 +589,7 @@
             field[c] = field[c] + total[c * lines : (c + 1) * lines]
 
     field[...] = jnp.zeros_like(field)
-    repeat(patches, scatter_patch, 4)
+    repeat(patches, scatter_patch, 8)
 
     for copy in flow_copies:
         copy.wait_recv()

time: 45 us -> 44.4 us (0.987)
    pallas_call x1, Pallas kernels: 39.7 us -> 39.3 us  [per_device(): pl.pallas_call(body, out_shape=(jax.ShapeDtypeStruct(populations.shape, F...]
where the time goes in v6:
time: 44.4 us; the launch traced here: 44.3 us
  Pallas kernels  39.3 us (89%)
  local copies, waits for them, and re-layouts  4.39 us (10%)
  between operations  0.64 us (1%)
    pallas_call x1, Pallas kernels, per_device(): pl.pallas_call(body, out_shape=(jax.ShapeDtypeStruct(populations.shape, F...  39.3 us
    unnamed x4, local copies, waits for them, and re-layouts  4.39 us

profile of v6, /device:TPU:1, one launch (start us, length us, event | category | flops | bytes accessed | tf_op | source)
XLA Modules:
  0.0 44.3 jit_solution(3023621230944873170)
XLA Ops:
  0.6 39.3 %shard_map.111 = (f32[19,4,64,256]{3,2,1,0:T(8,128)S(1)}, f32[3,8,512]{2,1,0:T(8,128)S(1)}, f32[3,8,512]{2,1,0:T(8,128)S(1)}, f32[3,256,256]{2,1,0:T(8,128)S(1)}) custom-call(s32[8,2,8]{2,1,0:T(2,128)} %bitcast.11, s32[8]{0:T(128)} %refs_1_.1, f32[19,4,64,256]{3,2,1,0:T(8,128)} %refs_2_.1, s32[4,64,256]{2,1,0:T(8,128)} %refs_3_.1, s32[8,512]{1,0:T(8,128)} %refs_4_.1, ...), custom_call_target="tpu_custom_call" | custom-call | tf_op jit(solution)/shard_map/pallas_call | solution.py:626
  39.9 2.3 %copy.16 = f32[19,4,64,256]{3,2,1,0:T(8,128)} copy(f32[19,4,64,256]{3,2,1,0:T(8,128)S(1)} %get-tuple-element.16) | data formatting | bytes 9961472
  42.2 0.6 %copy.17 = f32[8,3,512]{2,0,1:T(8,128)} copy(f32[8,3,512]{2,0,1:T(8,128)S(1)} %bitcast.8) | data formatting | bytes 98304
  42.8 0.6 %copy.18 = f32[8,3,512]{2,0,1:T(8,128)} copy(f32[8,3,512]{2,0,1:T(8,128)S(1)} %bitcast.7) | data formatting | bytes 98304
  43.4 0.9 %copy.19 = f32[3,4,64,256]{3,2,1,0:T(8,128)} copy(f32[3,4,64,256]{3,2,1,0:T(8,128)S(1)} %bitcast.6) | data formatting | bytes 1572864
